TPU v7x, 32 devices: a whole 2x2x4 slice. The times are simulated.
32 devices in a mesh: tm: 8 (over z, x), rows: 4 (over y, core).
Axes of the slice: x: 2, y: 2, z: 4, core: 2. Of those that a mesh axis runs over, the one named last changes fastest.
Arguments:
- frames: bfloat16 [4, 24576, 512], P('rows', 'tm'), may hold values from -6 to 6
- cotangent: bfloat16 [4, 24576, 512], P('rows', 'tm'), may hold values from -6 to 6
- lengths: int32 [4, 80], P('rows'), may hold values from 0 to 2816, as said below
- w1_master: float32 [512, 1536], P('tm'), may hold values from -0.25 to 0.25
- w1_first: float32 [512, 1536], P('tm'), may hold values from -512 to 512
- w1_second: float32 [512, 1536], P('tm'), may hold values from 4423.68 to 70778.88
- w1_average: float32 [512, 1536], P('tm'), may hold values from -0.25 to 0.25
- w2_master: float32 [1536, 512], P('tm'), may hold values from -0.15625 to 0.15625
- w2_first: float32 [1536, 512], P('tm'), may hold values from -1024 to 1024
- w2_second: float32 [1536, 512], P('tm'), may hold values from 17694.72 to 283115.53
- w2_average: float32 [1536, 512], P('tm'), may hold values from -0.15625 to 0.15625
- small_master: float32 [15, 512], replicated, may hold values from -0.6 to 1.3
- small_first: float32 [15, 512], replicated, may hold values from -896 to 896
- small_second: float32 [15, 512], replicated, may hold values from 12288 to 196608
- small_average: float32 [15, 512], replicated, may hold values from -0.6 to 1.3
Outputs:
- output: bfloat16 [4, 24576, 512], P('rows', 'tm')
- input_grad: bfloat16 [4, 24576, 512], P('rows', 'tm')
- w1_new: float32 [512, 1536], P('tm')
- w1_first_new: float32 [512, 1536], P('tm')
- w1_second_new: float32 [512, 1536], P('tm')
- w1_average_new: float32 [512, 1536], P('tm')
- w1_copy: bfloat16 [512, 1536], P('tm')
- w2_new: float32 [1536, 512], P('tm')
- w2_first_new: float32 [1536, 512], P('tm')
- w2_second_new: float32 [1536, 512], P('tm')
- w2_average_new: float32 [1536, 512], P('tm')
- w2_copy: bfloat16 [1536, 512], P('tm')
- small_new: float32 [15, 512], replicated
- small_first_new: float32 [15, 512], replicated
- small_second_new: float32 [15, 512], replicated
- small_average_new: float32 [15, 512], replicated
- small_copy: bfloat16 [15, 512], replicated
Inputs may be any that keep to these rules, and one draw needn't show every extreme that they name: `lengths`: each row sums to 24576 frames; every nonzero entry is 128, 1024 or 2816, and every row holds a clip of exactly 2816 frames.
All inputs are finite; a program needn't handle non-finite values.
Results may differ from a plain program's by a relative error of at most 0.013.
Values may be sent and summed in bfloat16 or wider, within the bound.
A program may use at most 192 MiB of HBM per device.

v0:
```python
import jax
import jax.numpy as jnp
from jax import lax
from jax.sharding import PartitionSpec as P

ADAM_STEP = 3


norm_eps = 1e-06
adam_eps = 1e-08
weight_decay = 0.01
beta_first = 0.5
beta_second = 0.5
average_keep = 0.75
rate_first = 0.08
rate_second = 0.05
rate_small = 0.4


def padded_2(array, sides, width):
    for axis, dim in sides:
        devices, length = (lax.axis_size(axis), array.shape[dim])
        up = [(i, (i + 1) % devices) for i in range(devices - 1)]
        down = [(j, i) for i, j in up]
        last = lax.slice_in_dim(array, length - width, length, axis=dim)
        leading = lax.slice_in_dim(array, 0, width, axis=dim)
        before = lax.ppermute(last, axis, up)
        after = lax.ppermute(leading, axis, down)
        array = jnp.concatenate([before, array, after], axis=dim)
    return array


def cut_along(array, dim, devices):
    before, after = (array.shape[:dim], array.shape[dim + 1 :])
    return jnp.moveaxis(array.reshape(*before, devices, -1, *after), dim, 0)


def sent_and_summed(array, axis, dim):
    devices = lax.axis_size(axis)
    pieces = lax.all_to_all(cut_along(array, dim, devices), axis, 0, 0, tiled=True)
    return jnp.sum(pieces.astype(jnp.float32), axis=0)


def edge_masks(lengths_row, first_frame, frame_count):
    ends_at = jnp.cumsum(lengths_row, dtype=jnp.int32)
    places = first_frame + jnp.arange(frame_count, dtype=jnp.int32)
    passed = ends_at[None, :] <= places[:, None]
    lower = jnp.max(jnp.where(passed, ends_at[None, :], 0), axis=1)
    upper = jnp.min(jnp.where(passed, ends_at[-1], ends_at[None, :]), axis=1)
    mask_rows = []
    for tap_index in range(7):
        spot_now = places + (tap_index - 3)
        mask_rows.append(((spot_now >= lower) & (spot_now < upper)).astype(jnp.float32))
    return jnp.stack(mask_rows)


def depthwise(padded, tap_rows, masks, frame_count):
    summed = jnp.zeros((frame_count, padded.shape[1]), jnp.float32)
    for tap_index in range(7):
        window = padded[tap_index : tap_index + frame_count].astype(jnp.float32)
        summed = summed + tap_rows[tap_index][None, :] * window * masks[tap_index][:, None]
    return summed


def layer_norm(conv_out, norm_gain, norm_bias):
    centred = conv_out - jnp.mean(conv_out, axis=-1, keepdims=True)
    spread = jnp.mean(centred * centred, axis=-1, keepdims=True)
    return centred * lax.rsqrt(spread + norm_eps) * norm_gain[None, :] + norm_bias[None, :]


def exact_gelu(values):
    return jax.nn.gelu(values, approximate=False)


def adamw_step(master, first_old, second_old, average_old, gradient, rate):
    first_new = beta_first * first_old + (1.0 - beta_first) * gradient
    second_new = beta_second * second_old + (1.0 - beta_second) * gradient * gradient
    first_hat = first_new / (1.0 - beta_first**ADAM_STEP)
    second_hat = second_new / (1.0 - beta_second**ADAM_STEP)
    master_new = master - rate * (
        first_hat / (jnp.sqrt(second_hat) + adam_eps) + weight_decay * master
    )
    average_new = average_keep * average_old + (1.0 - average_keep) * master_new
    return (master_new, first_new, second_new, average_new, master_new.astype(jnp.bfloat16))


def frame_product(left_side, right_side):
    return lax.dot_general(
        left_side, right_side, (((0,), (0,)), ((), ())), preferred_element_type=jnp.float32
    )


def body(
    frames,
    cotangent,
    lengths,
    w1_master,
    w1_first,
    w1_second,
    w1_average,
    w2_master,
    w2_first,
    w2_second,
    w2_average,
    small_master,
    small_first,
    small_second,
    small_average,
):
    frame_count = frames.shape[1]
    width = frames.shape[2]
    w1_low, w2_low = (
        lax.all_gather(w1_master.astype(jnp.bfloat16), "tm", axis=0, tiled=True),
        lax.all_gather(w2_master.astype(jnp.bfloat16), "tm", axis=0, tiled=True),
    )
    inputs = frames[0]
    upstream = cotangent[0].astype(jnp.float32)
    masks = edge_masks(lengths[0], lax.axis_index("tm") * frame_count, frame_count)
    tap_rows = small_master[0:7]
    layer_scale = small_master[14]
    padded = padded_2(inputs, (("tm", 0),), 3)
    conv_out = depthwise(padded, tap_rows, masks, frame_count) + small_master[7][None, :]
    normed, norm_back = jax.vjp(layer_norm, conv_out, small_master[8], small_master[9])
    normed_low = normed.astype(jnp.bfloat16)
    hidden = (
        jnp.dot(normed_low, w1_low, preferred_element_type=jnp.float32)
        + small_master[10:13].reshape(-1)[None, :]
    )
    activated, gelu_back = jax.vjp(exact_gelu, hidden)
    act_low = activated.astype(jnp.bfloat16)
    branch = (
        jnp.dot(act_low, w2_low, preferred_element_type=jnp.float32) + small_master[13][None, :]
    )
    output = (inputs.astype(jnp.float32) + layer_scale[None, :] * branch).astype(jnp.bfloat16)
    grad_scale = jnp.sum(upstream * branch, axis=0)
    grad_branch = (layer_scale[None, :] * upstream).astype(jnp.bfloat16)
    grad_act = lax.dot_general(
        grad_branch, w2_low, (((1,), (1,)), ((), ())), preferred_element_type=jnp.float32
    )
    grad_hidden = gelu_back(grad_act)[0].astype(jnp.bfloat16)
    grad_normed = lax.dot_general(
        grad_hidden, w1_low, (((1,), (1,)), ((), ())), preferred_element_type=jnp.float32
    )
    grad_conv, grad_gain, grad_shift = norm_back(grad_normed)
    grad_low = grad_conv.astype(jnp.bfloat16)
    grad_pad = padded_2(grad_low, (("tm", 0),), 3)
    input_grad = (upstream + depthwise(grad_pad, tap_rows[::-1], masks, frame_count)).astype(
        jnp.bfloat16
    )
    grad_float = grad_low.astype(jnp.float32)
    grad_taps = jnp.stack(
        [
            jnp.sum(
                grad_float
                * padded[tap_index : tap_index + frame_count].astype(jnp.float32)
                * masks[tap_index][:, None],
                axis=0,
            )
            for tap_index in range(7)
        ]
    )
    middle_rows = jnp.stack([jnp.sum(grad_float, axis=0), grad_gain, grad_shift])
    bias_rows = jnp.sum(grad_hidden.astype(jnp.float32), axis=0).reshape(3, width)
    last_rows = jnp.stack([jnp.sum(grad_branch.astype(jnp.float32), axis=0), grad_scale])
    small_grad = jnp.concatenate([grad_taps, middle_rows, bias_rows, last_rows], axis=0)
    full_one = frame_product(normed_low, grad_hidden)
    full_two = frame_product(act_low, grad_branch)
    share_one, share_two = (
        sent_and_summed(full_one.astype(jnp.bfloat16), "tm", 0),
        sent_and_summed(full_two.astype(jnp.bfloat16), "tm", 0),
    )
    grad_one, grad_two = (
        lax.psum(share_one.astype(jnp.bfloat16), "rows").astype(jnp.float32),
        lax.psum(share_two.astype(jnp.bfloat16), "rows").astype(jnp.float32),
    )
    small_total = lax.psum(small_grad, ("tm", "rows"))
    one_out = adamw_step(w1_master, w1_first, w1_second, w1_average, grad_one, rate_first)
    two_out = adamw_step(w2_master, w2_first, w2_second, w2_average, grad_two, rate_second)
    small_out = adamw_step(
        small_master, small_first, small_second, small_average, small_total, rate_small
    )
    return (
        output[None],
        input_grad[None],
        one_out[0],
        one_out[1],
        one_out[2],
        one_out[3],
        one_out[4],
        two_out[0],
        two_out[1],
        two_out[2],
        two_out[3],
        two_out[4],
        small_out[0],
        small_out[1],
        small_out[2],
        small_out[3],
        small_out[4],
    )


def solution(mesh):
    in_specs = (
        P("rows", "tm", None),
        P("rows", "tm", None),
        P("rows", None),
        P("tm", None),
        P("tm", None),
        P("tm", None),
        P("tm", None),
        P("tm", None),
        P("tm", None),
        P("tm", None),
        P("tm", None),
        P(),
        P(),
        P(),
        P(),
    )
    out_specs = (
        P("rows", "tm", None),
        P("rows", "tm", None),
        P("tm", None),
        P("tm", None),
        P("tm", None),
        P("tm", None),
        P("tm", None),
        P("tm", None),
        P("tm", None),
        P("tm", None),
        P("tm", None),
        P("tm", None),
        P(),
        P(),
        P(),
        P(),
        P(),
    )
    return jax.shard_map(body, mesh=mesh, in_specs=in_specs, out_specs=out_specs, check_vma=False)
```

profile of v0, /device:TPU:0, one launch (start us, length us, event | category | flops | bytes accessed | tf_op | source)
XLA Modules:
  0.0 309.7 jit_solution(15408385208121111069)
XLA Ops:
  9.7 4.8 %collective-permute-start = (bf16[3,512]{1,0:T(4,128)(2,1)S(1)}, bf16[3,512]{1,0:T(4,128)(2,1)S(1)}, u32[]{:S(2)}, u32[]{:S(2)}) collective-permute-start(bf16[3,512]{1,0:T(4,128)(2,1)S(1)} %get-tuple-element.61), channel_id=1, source_target_pairs={{0,4},{4,8},{8,12},{12,16},{16,20},{20,24},{24,28},{1,5},{5,9},{9,... | collective-permute-start | bytes 9224 | tf_op jit(solution)/shard_map/ppermute | solution.py:27
  22.7 19.7 %fusion.107 = (f32[3072]{0:T(1024)S(1)}, f32[3072,512]{1,0:T(8,128)S(1)}) fusion(f32[512]{0:T(512)S(1)} %bitcast.101, f32[3072]{0:T(1024)S(1)} %get-tuple-element.76, bf16[3,512]{1,0:T(4,128)(2,1)S(1)} %collective-permute-done.1, bf16[3072,512]{1,0:T(8,128)(2,1)} %bitcast.65, f32[512]{0:T(512)S(1)} %bitcast.69, f32[3072]{0:T(1024)S(1)} %get-tuple-element.77, ...), kind=kLoop, calls=%fused_computation.173 | loop fusion | flops 73921536 | bytes 9558016 | tf_op jit(solution)/shard_map/jvp()/reduce_sum | solution.py:66
  42.4 2.5 copy-done
  47.2 10.5 %all-gather.3.cloned.1.call-done = bf16[512,1536]{1,0:T(8,128)(2,1)} async-done(((bf16[64,1536]{1,0:T(8,128)(2,1)}), bf16[512,1536]{1,0:T(8,128)(2,1)}) %all-gather.3.cloned.1.call-update) | async-done | bytes 1572880 | tf_op jit(solution)/shard_map/all_gather | solution.py:113
  57.7 49.9 %multiply_convert_fusion = (bf16[3072,1536]{1,0:T(8,128)(2,1)}, f32[3072,1536]{1,0:T(8,128)}, f32[3072,1536]{1,0:T(8,128)}) fusion(f32[1536]{0:T(1024)S(1)} %add.274, bf16[512,1536]{1,0:T(8,128)(2,1)} %all-gather.3.cloned.1.call-done, f32[3072,512]{1,0:T(8,128)} %copy-done, f32[512]{0:T(512)S(1)} %bitcast.104, f32[512]{0:T(512)S(1)} %bitcast.94, ...), kind=kOutput, calls=%fused_computation.13 | convolution fusion | flops 5151129600 | bytes 55085056 | tf_op jit(solution)/shard_map/dot_general | solution.py:126
  107.6 21.4 %convert_reduce_fusion = (f32[1536]{0:T(1024)S(1)}, bf16[3072,1536]{1,0:T(8,128)(2,1)}) fusion(f32[3072,1536]{1,0:T(8,128)} %get-tuple-element.53, bf16[1536,512]{1,0:T(8,128)(2,1)} %all-gather.5.cloned.1.call-done, bf16[1,3072,512]{2,1,0:T(8,128)(2,1)S(1)} %copy-done.4, f32[512]{0:T(512)S(1)} %bitcast.90, f32[3072,1536]{1,0:T(8,128)} %get-tuple-element.82, ...), kind=kOutput, calls=%fused_computation.2 | convolution fusion | flops 4916771328 | bytes 51918848 | tf_op jit(solution)/shard_map/dot_general | solution.py:137
  129.1 10.3 %convolution_convert_fusion.1 = bf16[512,1536]{1,0:T(8,128)(2,1)} fusion(bf16[3072,1536]{1,0:T(8,128)(2,1)} %get-tuple-element.85, f32[3072,512]{1,0:T(8,128)S(1)} %copy-done.1, f32[512]{0:T(512)S(1)} %bitcast.105, f32[512]{0:T(512)S(1)} %bitcast.95, f32[3072]{0:T(1024)S(1)} %fusion.97, f32[3072]{0:T(1024)S(1)} %broadcast_multiply_fusion), kind=kOutput, calls=%fused_computation.105 | convolution fusion | flops 4840488960 | bytes 17330176 | tf_op jit(solution)/shard_map/dot_general | solution.py:88
  139.4 4.4 %all-to-all-start = ((bf16[8,64,1536]{2,1,0:T(8,128)(2,1)}), bf16[8,64,1536]{2,1,0:T(8,128)(2,1)}, u32[]{:S(2)}, u32[]{:S(2)}) async-start(bf16[8,64,1536]{2,1,0:T(8,128)(2,1)} %bitcast.68), calls=%async_computation | async-start | bytes 3145728 | tf_op jit(solution)/shard_map/all_to_all | solution.py:40
  143.8 10.6 %convolution_convert_fusion = bf16[1536,512]{1,0:T(8,128)(2,1)} fusion(bf16[3072,1536]{1,0:T(8,128)(2,1)} %get-tuple-element.52, bf16[1,3072,512]{2,1,0:T(8,128)(2,1)} %param.16, f32[512]{0:T(512)S(1)} %bitcast.91), kind=kOutput, calls=%fused_computation.104 | convolution fusion | flops 4837343232 | bytes 14157824 | tf_op jit(solution)/shard_map/dot_general | solution.py:88
  154.5 8.7 %multiply_reduce_fusion = (f32[512]{0:T(512)S(1)}, f32[3072]{0:T(1024)S(1)}, f32[512]{0:T(512)S(1)}, f32[3072,512]{1,0:T(8,128)S(1)}) fusion(f32[3072,512]{1,0:T(8,128)S(1)} %bitcast.64, f32[3072]{0:T(1024)S(1)} %fusion.97, f32[3072]{0:T(1024)S(1)} %broadcast_multiply_fusion, f32[512]{0:T(512)S(1)} %bitcast.96, bf16[3072,1536]{1,0:T(8,128)(2,1)} %get-tuple-element.85, ...), kind=kOutput, calls=%fused_computation.77 | convolution fusion | flops 4844417024 | bytes 23635968 | tf_op jit(solution)/shard_map/dot_general | solution.py:141
  163.3 4.4 %fusion.105 = (f32[3072]{0:T(1024)S(1)}, f32[3072,512]{1,0:T(8,128)}) fusion(f32[3072]{0:T(1024)S(1)} %multiply_multiply_fusion.8, f32[3072,512]{1,0:T(8,128)S(1)} %bitcast.64, f32[3072]{0:T(1024)S(1)} %broadcast_multiply_fusion, f32[3072]{0:T(1024)S(1)} %fusion.97, f32[3072,512]{1,0:T(8,128)S(1)} %get-tuple-element.83, f32[512]{0:T(512)S(1)} %bitcast.97), kind=kLoop, calls=%fused_computation.172 | loop fusion | flops 11006976 | bytes 18925568 | tf_op jit(solution)/shard_map/transpose(jvp())/reduce_sum | solution.py:66
  167.8 7.0 %fusion.111 = f32[3072,512]{1,0:T(8,128)} fusion(bf16[3072,1536]{1,0:T(8,128)(2,1)S(1)} %bitcast.108, bf16[1536,512]{1,0:T(8,128)(2,1)S(1)} %copy-done.44), kind=kOutput, calls=%fused_computation.176 | convolution fusion | flops 4831838208 | bytes 17301504 | tf_op jit(solution)/shard_map/dot_general | solution.py:132
  174.8 5.7 %all-to-all-done = bf16[8,64,1536]{2,1,0:T(8,128)(2,1)} async-done(((bf16[8,64,1536]{2,1,0:T(8,128)(2,1)}), bf16[8,64,1536]{2,1,0:T(8,128)(2,1)}, u32[]{:S(2)}, u32[]{:S(2)}) %all-to-all-start) | async-done | bytes 1572896 | tf_op jit(solution)/shard_map/all_to_all | solution.py:40
  180.5 4.3 %all-to-all-start.1 = ((bf16[8,192,512]{2,1,0:T(8,128)(2,1)}), bf16[8,192,512]{2,1,0:T(8,128)(2,1)}, u32[]{:S(2)}, u32[]{:S(2)}) async-start(bf16[8,192,512]{2,1,0:T(8,128)(2,1)} %bitcast.67), calls=%async_computation.1 | async-start | bytes 3145728 | tf_op jit(solution)/shard_map/all_to_all | solution.py:40
  185.0 10.2 %fusion.23 = (f32[512]{0:T(512)S(1)}, f32[512]{0:T(512)S(1)}, bf16[1,3072,512]{2,1,0:T(8,128)(2,1)}, f32[512]{0:T(512)S(1)}, bf16[3072,512]{1,0:T(8,128)(2,1)}) fusion(f32[3072,512]{1,0:T(8,128)} %fusion.111, bf16[1,3072,512]{2,1,0:T(8,128)(2,1)} %param.16, f32[512]{0:T(512)S(1)} %bitcast.93, f32[512]{0:T(512)S(1)} %bitcast.92, ...), kind=kLoop, calls=%fused_computation.56 | loop fusion | flops 28310016 | bytes 25200640 | tf_op jit(solution)/shard_map/reduce_sum | solution.py:135
  196.6 4.3 %collective-permute-start.2 = (bf16[3,512]{1,0:T(4,128)(2,1)}, bf16[3,512]{1,0:T(4,128)(2,1)}, u32[]{:S(2)}, u32[]{:S(2)}) collective-permute-start(bf16[3,512]{1,0:T(4,128)(2,1)} %get-tuple-element.59), channel_id=1, source_target_pairs={{0,4},{4,8},{8,12},{12,16},{16,20},{20,24},{24,28},{1,5},{5,9},{9,... | collective-permute-start | bytes 9224 | tf_op jit(solution)/shard_map/ppermute | solution.py:27
  202.2 12.6 %fusion.42 = (f32[512]{0:T(512)S(1)}, f32[512]{0:T(512)S(1)}, f32[512]{0:T(512)S(1)}, f32[512]{0:T(512)S(1)}, f32[512]{0:T(512)S(1)}, /*index=5*/f32[512]{0:T(512)S(1)}, f32[512]{0:T(512)S(1)}) fusion(bf16[3072,512]{1,0:T(8,128)(2,1)} %get-tuple-element.58, bf16[3,512]{1,0:T(4,128)(2,1)S(1)} %copy-done.41, bf16[3072,512]{1,0:T(8,128)(2,1)S(1)} %bitcast.66, ...), kind=kLoop, calls=%fused_computation.75 | loop fusion | flops 69202432 | bytes 6385664 | tf_op jit(solution)/shard_map/reduce_sum | solution.py:153
  215.0 41.0 %psum.23 = f32[15,512]{1,0:T(8,128)S(1)} all-reduce(f32[15,512]{1,0:T(8,128)S(1)} %concatenate.29), channel_id=1, replica_groups=mesh['tm'=8,'rows'=4] {'tm','rows'}, use_global_device_ids=true, to_apply=%region_24.25 | all-reduce | flops 7680 | bytes 61440 | tf_op jit(solution)/shard_map/psum | solution.py:176
  257.3 2.4 reduce_sum.197
  259.6 2.4 reduce_sum.198
  262.1 15.3 %fusion.52 = bf16[1,3072,512]{2,1,0:T(8,128)(2,1)} fusion(f32[3072]{0:T(1024)} %copy-done.11, bf16[3,512]{1,0:T(4,128)(2,1)} %collective-permute-done.3, bf16[3072,512]{1,0:T(8,128)(2,1)S(1)} %copy-done.3, f32[512]{0:T(512)} %bitcast.82, f32[3072]{0:T(1024)} %copy-done.13, f32[512]{0:T(512)} %bitcast.80, f32[3072]{0:T(1024)} %copy-done.15, f32[512]{0:T(512)} %bitcast.78, ...), kind=kLoop, calls=%fused_computation.103 | loop fusion | flops 75497472 | bytes 9543680 | tf_op jit(solution)/shard_map/broadcast_in_dim | solution.py:184
  277.4 18.2 %all-reduce.3.cloned.1.call-done = (bf16[64,1536]{1,0:T(8,128)(2,1)}, bf16[192,512]{1,0:T(8,128)(2,1)}) async-done(((bf16[64,1536]{1,0:T(8,128)(2,1)}, bf16[192,512]{1,0:T(8,128)(2,1)}), (bf16[64,1536]{1,0:T(8,128)(2,1)}, bf16[192,512]{1,0:T(8,128)(2,1)})) %all-reduce.3.cloned.1.call-update) | async-done | bytes 393232 | tf_op jit(solution)/shard_map/psum | solution.py:173
  295.6 2.3 fusion.103
  299.9 2.5 fusion.101
  (140 shorter events, 19.6 us)
Async XLA Ops:
  7.2 50.5 %all-gather.3.cloned.1.call-start = ((), (), s32[]{:S(2)}) async-start(), calls=%async_computation.2 | async-start | bytes 1769472 | tf_op jit(solution)/shard_map/all_gather | solution.py:113
  9.0 98.7 %all-gather.5.cloned.1.call-start = ((), (), s32[]{:S(2)}) async-start(), calls=%async_computation.3 | async-start | bytes 1769472 | tf_op jit(solution)/shard_map/all_gather | solution.py:114
  9.7 12.9 %collective-permute-start = (bf16[3,512]{1,0:T(4,128)(2,1)S(1)}, bf16[3,512]{1,0:T(4,128)(2,1)S(1)}, u32[]{:S(2)}, u32[]{:S(2)}) collective-permute-start(bf16[3,512]{1,0:T(4,128)(2,1)S(1)} %get-tuple-element.61), channel_id=1, source_target_pairs={{0,4},{4,8},{8,12},{12,16},{16,20},{20,24},{24,28},{1,5},{5,9},{9,... | collective-permute-start | bytes 9224 | tf_op jit(solution)/shard_map/ppermute | solution.py:27
  14.6 8.1 %collective-permute-start.1 = (bf16[3,512]{1,0:T(4,128)(2,1)S(1)}, bf16[3,512]{1,0:T(4,128)(2,1)S(1)}, u32[]{:S(2)}, u32[]{:S(2)}) collective-permute-start(bf16[3,512]{1,0:T(4,128)(2,1)S(1)} %get-tuple-element.62), channel_id=1, source_target_pairs={{4,0},{8,4},{12,8},{16,12},{20,16},{24,20},{28,24},{5,1},{9,5},{13... | collective-permute-start | bytes 9224 | tf_op jit(solution)/shard_map/ppermute | solution.py:28
  20.1 26.9 %copy-start.9 = (f32[3072]{0:T(1024)}, f32[3072]{0:T(1024)S(1)}, u32[]{:S(2)}) copy-start(f32[3072]{0:T(1024)S(1)} %get-tuple-element.75) | copy-start | bytes 36868
  20.1 26.9 %copy-start.11 = (f32[3072]{0:T(1024)}, f32[3072]{0:T(1024)S(1)}, u32[]{:S(2)}) copy-start(f32[3072]{0:T(1024)S(1)} %get-tuple-element.76) | copy-start | bytes 36868
  20.2 26.9 %copy-start.13 = (f32[3072]{0:T(1024)}, f32[3072]{0:T(1024)S(1)}, u32[]{:S(2)}) copy-start(f32[3072]{0:T(1024)S(1)} %get-tuple-element.77) | copy-start | bytes 36868
  20.2 26.9 %copy-start.15 = (f32[3072]{0:T(1024)}, f32[3072]{0:T(1024)S(1)}, u32[]{:S(2)}) copy-start(f32[3072]{0:T(1024)S(1)} %get-tuple-element.78) | copy-start | bytes 36868
  20.2 26.9 %copy-start.17 = (f32[3072]{0:T(1024)}, f32[3072]{0:T(1024)S(1)}, u32[]{:S(2)}) copy-start(f32[3072]{0:T(1024)S(1)} %get-tuple-element.79) | copy-start | bytes 36868
  20.2 26.9 %copy-start.19 = (f32[3072]{0:T(1024)}, f32[3072]{0:T(1024)S(1)}, u32[]{:S(2)}) copy-start(f32[3072]{0:T(1024)S(1)} %get-tuple-element.80) | copy-start | bytes 36868
  20.2 26.9 %copy-start.21 = (f32[3072]{0:T(1024)}, f32[3072]{0:T(1024)S(1)}, u32[]{:S(2)}) copy-start(f32[3072]{0:T(1024)S(1)} %get-tuple-element.81) | copy-start | bytes 36868
  57.7 49.9 %copy-start.4 = (bf16[1,3072,512]{2,1,0:T(8,128)(2,1)S(1)}, bf16[1,3072,512]{2,1,0:T(8,128)(2,1)}, u32[]{:S(2)}) copy-start(bf16[1,3072,512]{2,1,0:T(8,128)(2,1)} %param.16) | copy-start | bytes 9437188
  139.4 41.1 %all-to-all-start = ((bf16[8,64,1536]{2,1,0:T(8,128)(2,1)}), bf16[8,64,1536]{2,1,0:T(8,128)(2,1)}, u32[]{:S(2)}, u32[]{:S(2)}) async-start(bf16[8,64,1536]{2,1,0:T(8,128)(2,1)} %bitcast.68), calls=%async_computation | async-start | bytes 3145728 | tf_op jit(solution)/shard_map/all_to_all | solution.py:40
  180.5 79.2 %all-to-all-start.1 = ((bf16[8,192,512]{2,1,0:T(8,128)(2,1)}), bf16[8,192,512]{2,1,0:T(8,128)(2,1)}, u32[]{:S(2)}, u32[]{:S(2)}) async-start(bf16[8,192,512]{2,1,0:T(8,128)(2,1)} %bitcast.67), calls=%async_computation.1 | async-start | bytes 3145728 | tf_op jit(solution)/shard_map/all_to_all | solution.py:40
  184.8 110.8 %all-reduce.3.cloned.1.call-start = ((), (), s32[]{:S(2)}) async-start(), calls=%async_computation.4 | async-start | bytes 786432 | tf_op jit(solution)/shard_map/psum | solution.py:173
  195.2 60.8 %copy-start.23 = (f32[15,512]{1,0:T(8,128)S(1)}, f32[15,512]{1,0:T(8,128)}, u32[]{:S(2)}) copy-start(f32[15,512]{1,0:T(8,128)} %param.26) | copy-start | bytes 92164
  195.2 60.8 %copy-start.27 = (f32[15,512]{1,0:T(8,128)S(1)}, f32[15,512]{1,0:T(8,128)}, u32[]{:S(2)}) copy-start(f32[15,512]{1,0:T(8,128)} %param.27) | copy-start | bytes 92164
  195.2 60.8 %copy-start.28 = (f32[15,512]{1,0:T(8,128)S(1)}, f32[15,512]{1,0:T(8,128)}, u32[]{:S(2)}) copy-start(f32[15,512]{1,0:T(8,128)} %param.28) | copy-start | bytes 92164
  195.2 61.4 %copy-start.29 = (f32[15,512]{1,0:T(8,128)S(1)}, f32[15,512]{1,0:T(8,128)}, u32[]{:S(2)}) copy-start(f32[15,512]{1,0:T(8,128)} %param.29) | copy-start | bytes 92164
  195.2 66.9 %copy-start.31 = (f32[1,512]{1,0:T(1,128)S(1)}, f32[1,512]{1,0:T(1,128)}, u32[]{:S(2)}) copy-start(f32[1,512]{1,0:T(1,128)} %copy-done.30) | copy-start | bytes 6148
  196.6 65.5 %collective-permute-start.2 = (bf16[3,512]{1,0:T(4,128)(2,1)}, bf16[3,512]{1,0:T(4,128)(2,1)}, u32[]{:S(2)}, u32[]{:S(2)}) collective-permute-start(bf16[3,512]{1,0:T(4,128)(2,1)} %get-tuple-element.59), channel_id=1, source_target_pairs={{0,4},{4,8},{8,12},{12,16},{16,20},{20,24},{24,28},{1,5},{5,9},{9,... | collective-permute-start | bytes 9224 | tf_op jit(solution)/shard_map/ppermute | solution.py:27
  200.9 61.2 %collective-permute-start.3 = (bf16[3,512]{1,0:T(4,128)(2,1)}, bf16[3,512]{1,0:T(4,128)(2,1)}, u32[]{:S(2)}, u32[]{:S(2)}) collective-permute-start(bf16[3,512]{1,0:T(4,128)(2,1)} %get-tuple-element.60), channel_id=1, source_target_pairs={{4,0},{8,4},{12,8},{16,12},{20,16},{24,20},{28,24},{5,1},{9,5},{13... | collective-permute-start | bytes 9224 | tf_op jit(solution)/shard_map/ppermute | solution.py:28
  214.9 47.2 %copy-start.3 = (bf16[3072,512]{1,0:T(8,128)(2,1)S(1)}, bf16[3072,512]{1,0:T(8,128)(2,1)}, u32[]{:S(2)}) copy-start(bf16[3072,512]{1,0:T(8,128)(2,1)} %get-tuple-element.58) | copy-start | bytes 9437188
  259.6 36.0 %copy-start.5 = (f32[64,1536]{1,0:T(8,128)S(1)}, f32[64,1536]{1,0:T(8,128)}, u32[]{:S(2)}) copy-start(f32[64,1536]{1,0:T(8,128)} %param.18) | copy-start | bytes 1179652
  (35 other events, 562.4 us)
Sparse Core Ops, SparseCore 0:
  10.8 46.8 all-gather.2
  60.4 43.0 all-gather.4
  262.2 33.4 all-reduce.2
where the time goes:
time: 311 us; the launch traced here: 310 us
  matrix products  108 us (35%)
  other arithmetic  82.7 us (27%)
  blocking collectives  41 us (13%)
  waiting for transfers between devices  34.4 us (11%)
  starting transfers between devices  20.6 us (7%)
  between operations  14.5 us (5%)
  local copies, waits for them, and re-layouts  8.58 us (3%)
    dot_general x1, matrix products, body(): jnp.dot(normed_low, w1_low, preferred_element_type=jnp.float32)  49.9 us
    psum x1, blocking collectives, body(): small_total = lax.psum(small_grad, ('tm', 'rows'))  41 us
    reduce_sum x2, other arithmetic, layer_norm(): centred = conv_out - jnp.mean(conv_out, axis=-1, keepdims=True)  24.2 us
    dot_general x1, matrix products, body(): lax.dot_general(grad_branch, w2_low, (((1,), (1,)), ((), ())), preferred_...  21.4 us
    dot_general x2, matrix products, frame_product(): lax.dot_general(left_side, right_side, (((0,), (0,)), ((), ())), preferre...  20.9 us
    psum x1, waiting for transfers between devices, body(): lax.psum(share_one.astype(jnp.bfloat16), 'rows').astype(jnp.float32)  18.2 us
    broadcast_in_dim x1, other arithmetic, body(): input_grad[None]  15.3 us
    reduce_sum x1, other arithmetic, body(): jnp.sum(grad_float * padded[tap_index:tap_index + frame_count].astype(jnp...  12.6 us
  transfers between devices with their start and end apart: 9, of which 3 were waited for; matrix products, arithmetic and copies ran while one was open for 50% of the time, Pallas kernels for 0%

commit v1 on v0

--- a/solution.py
+++ b/solution.py
@@ -1,11 +1,14 @@
+import functools
+
 import jax
 import jax.numpy as jnp
+import numpy as np
 from jax import lax
+from jax.experimental import pallas as pl
+from jax.experimental.pallas import tpu as pltpu
 from jax.sharding import PartitionSpec as P
 
 ADAM_STEP = 3
-
-
 norm_eps = 1e-06
 adam_eps = 1e-08
 weight_decay = 0.01
@@ -15,6 +18,756 @@
 rate_first = 0.08
 rate_second = 0.05
 rate_small = 0.4
+
+TAPS = 7
+TILE = 128
+GAP = 8
+GRAIN = 32
+HALO = 16
+F32 = jnp.float32
+BF16 = jnp.bfloat16
+MESH = pl.DeviceIdType.MESH
+RSQRT_HALF = np.float32(0.7071067811865476)
+RSQRT_2PI = np.float32(0.3989422804014327)
+
+
+def adamw_step(master, first_old, second_old, average_old, gradient, rate):
+    first_new = beta_first * first_old + (1.0 - beta_first) * gradient
+    second_new = beta_second * second_old + (1.0 - beta_second) * gradient * gradient
+    first_hat = first_new / (1.0 - beta_first**ADAM_STEP)
+    second_hat = second_new / (1.0 - beta_second**ADAM_STEP)
+    master_new = master - rate * (
+        first_hat / (jnp.sqrt(second_hat) + adam_eps) + weight_decay * master
+    )
+    average_new = average_keep * average_old + (1.0 - average_keep) * master_new
+    return (master_new, first_new, second_new, average_new, master_new.astype(BF16))
+
+
+class Plan:
+    def __init__(self, nt, nr, frame_count, width, hidden):
+        self.nt, self.nr, self.t, self.d, self.ff = nt, nr, frame_count, width, hidden
+        self.share = hidden // nt
+        self.rows1 = width // nt
+        self.part = self.rows1 // nr
+        self.lanes = width // nr
+        self.nb = frame_count // TILE
+        self.nc = width // 128
+        self.runs = [32, 64, 64, 32]
+        self.starts = [0, 32, 96, 160]
+        self.blocks = []
+        offset = 0
+        for run in self.runs:
+            self.blocks.append((offset, run * nt))
+            offset += run * nt
+        self.widest = max(size for _, size in self.blocks)
+        self.m = 1024
+        self.natural = []
+        for run, start in zip(self.runs, self.starts):
+            for k in range(nt):
+                for o in range(0, run, GRAIN):
+                    self.natural.append((self.share * k + start + o) // GRAIN)
+        self.regrouped = [self.natural.index(g) for g in range(hidden // GRAIN)]
+
+
+def lane_permuted(tile_of, source, count):
+    per = 128 // GRAIN
+    out = []
+    for tile in range(count):
+        value = None
+        for q in range(per):
+            run = source[tile * per + q]
+            piece = tile_of(run // per)
+            shift = ((q - run % per) % per) * GRAIN
+            if shift:
+                piece = pltpu.roll(piece, shift, 1)
+            if value is None:
+                value = piece
+            else:
+                lane = lax.broadcasted_iota(jnp.int32, piece.shape, 1)
+                value = jnp.where(lane >= q * GRAIN, piece, value)
+        out.append(value)
+    return out
+
+
+def fold(value):
+    rows = value.shape[0]
+    total = value[0:8]
+    for g in range(1, rows // 8):
+        total = total + value[8 * g : 8 * g + 8]
+    return total
+
+
+def kernel(
+    plan,
+    frames_hbm,
+    cot_hbm,
+    lengths_ref,
+    w1_hbm,
+    w2_hbm,
+    small_ref,
+    output_hbm,
+    ingrad_hbm,
+    g1_out,
+    g2_out,
+    small_out,
+    frx,
+    ct,
+    nm,
+    nmt,
+    gb,
+    gbt,
+    br,
+    gn,
+    xf,
+    xhat,
+    rstd,
+    w1b,
+    w2b,
+    m1,
+    m2,
+    acc1,
+    acc2,
+    lens,
+    flags,
+    b1p,
+    accs,
+    accb,
+    tmp,
+    s1w1,
+    s1w2,
+    r1w1,
+    r1w2,
+    s2w1,
+    s2w2,
+    r2w1,
+    r2w2,
+    s3w1,
+    s3w2,
+    r3w1,
+    r3w2,
+    finw1,
+    finw2,
+    sma,
+    smr,
+    smq,
+    smf,
+    hprev,
+    hnext,
+    in_sem,
+    out_sem,
+    send_sem,
+    halo_sem,
+    ag_sem,
+    rs_sem,
+    sm_sem,
+):
+    p = plan
+    nt, nr, t_len = p.nt, p.nr, p.t
+    me_t = lax.axis_index("tm")
+    me_r = lax.axis_index("rows")
+    near = me_r + 1 - 2 * (me_r % 2)
+    far = (me_r + 2) % nr
+    both = near + 2 - 4 * (near // 2)
+
+    def remote(src, dst, send, recv, tm=None, rows=None):
+        device = {"tm": me_t if tm is None else tm, "rows": me_r if rows is None else rows}
+        return pltpu.make_async_remote_copy(
+            src_ref=src, dst_ref=dst, send_sem=send, recv_sem=recv,
+            device_id=device, device_id_type=MESH,
+        )
+
+    def arrived(view, sem):
+        pltpu.make_async_copy(view, view, sem).wait()
+
+    loads = [
+        pltpu.make_async_copy(w1_hbm.at[pl.ds(pl.multiple_of(me_r * p.part, p.part), p.part)], m1, in_sem.at[0]),
+        pltpu.make_async_copy(w2_hbm.at[:, pl.ds(pl.multiple_of(me_r * p.lanes, p.lanes), p.lanes)], m2, in_sem.at[1]),
+        pltpu.make_async_copy(frames_hbm.at[0], frx.at[pl.ds(HALO, t_len)], in_sem.at[2]),
+        pltpu.make_async_copy(cot_hbm.at[0], ct, in_sem.at[3]),
+    ]
+    for load in loads:
+        load.start()
+
+    barrier = pltpu.get_barrier_semaphore()
+    for step in range(1, nt):
+        pl.semaphore_signal(
+            barrier, inc=1, device_id={"tm": (me_t + step) % nt, "rows": me_r}, device_id_type=MESH
+        )
+    for step in range(1, nr):
+        pl.semaphore_signal(
+            barrier, inc=1, device_id={"tm": me_t, "rows": (me_r + step) % nr}, device_id_type=MESH
+        )
+
+    lens[...] = jnp.zeros_like(lens)
+    n_len = lengths_ref.shape[1]
+    lens[0:1, 0:n_len] = lengths_ref[...].astype(F32)
+    ends = lens[...]
+    lane = lax.broadcasted_iota(jnp.int32, ends.shape, 1)
+    shift = 1
+    while shift < lens.shape[1]:
+        ends = ends + jnp.where(lane >= shift, pltpu.roll(ends, shift, 1), 0.0)
+        shift *= 2
+    n_flag = flags.shape[0]
+    spot = me_t * t_len + TILE * lax.broadcasted_iota(jnp.int32, (n_flag, lens.shape[1]), 0)
+    hit = (ends[0:1, :] == spot.astype(F32)) | (spot == 0)
+    edge = jnp.max(jnp.where(hit, 1.0, 0.0), axis=1, keepdims=True)
+    flags[...] = jnp.broadcast_to(edge, flags.shape)
+    accs[...] = jnp.zeros_like(accs)
+    accb[...] = jnp.zeros_like(accb)
+    bias_tiles = lane_permuted(
+        lambda i: jnp.broadcast_to(small_ref[10 + i // p.nc : 11 + i // p.nc, 128 * (i % p.nc) : 128 * (i % p.nc) + 128], (8, 128)),
+        p.natural,
+        p.ff // 128,
+    )
+    for i, tile in enumerate(bias_tiles):
+        b1p[:, 128 * i : 128 * i + 128] = tile
+
+    loads[0].wait()
+    loads[1].wait()
+    own1 = lane_permuted(lambda i: m1[:, 128 * i : 128 * i + 128], p.natural, p.ff // 128)
+    for i, tile in enumerate(own1):
+        w1b[me_t, me_r, :, 128 * i : 128 * i + 128] = tile.astype(BF16)
+    for (jo, _), run, start in zip(p.blocks, p.runs, p.starts):
+        w2b[me_r, pl.ds(pl.multiple_of(jo + run * me_t, run), run), :] = m2[start : start + run, :].astype(BF16)
+
+    pl.semaphore_wait(barrier, nt + nr - 2)
+
+    def halo_sends():
+        after, before = (me_t + 1) % nt, (me_t + nt - 1) % nt
+        return [
+            remote(frames_hbm.at[0, pl.ds(t_len - HALO, HALO)], frx.at[pl.ds(0, HALO)], send_sem.at[0], halo_sem.at[0], tm=after),
+            remote(frames_hbm.at[0, pl.ds(0, HALO)], frx.at[pl.ds(HALO + t_len, HALO)], send_sem.at[1], halo_sem.at[1], tm=before),
+        ]
+
+    def w1_part(j, q):
+        jo, size = p.blocks[j]
+        return w1b.at[:, q, :, pl.ds(jo, size)]
+
+    def w2_part(j, q):
+        jo, size = p.blocks[j]
+        return w2b.at[q, pl.ds(jo, size), :]
+
+    def spread_sends(j):
+        jo, size = p.blocks[j]
+        run = p.runs[j]
+        out = []
+        for step in range(1, nt):
+            peer = (me_t + step) % nt
+            one = w1b.at[me_t, me_r, :, pl.ds(jo, size)]
+            two = w2b.at[me_r, pl.ds(pl.multiple_of(jo + run * me_t, run), run), :]
+            out.append(remote(one, one, send_sem.at[2 + j], ag_sem.at[j, 0], tm=peer))
+            out.append(remote(two, two, send_sem.at[2 + j], ag_sem.at[j, 0], tm=peer))
+        return out
+
+    def spread_wait(j):
+        jo, size = p.blocks[j]
+        arrived(w1b.at[pl.ds(0, nt - 1), pl.ds(0, 2), :, pl.ds(jo, size)], ag_sem.at[j, 0])
+
+    def far_sends(j):
+        return [
+            remote(w1_part(j, me_r), w1_part(j, me_r), send_sem.at[6 + j], ag_sem.at[j, 1], rows=far),
+            remote(w2_part(j, me_r), w2_part(j, me_r), send_sem.at[6 + j], ag_sem.at[j, 1], rows=far),
+        ]
+
+    def far_wait(j):
+        jo, size = p.blocks[j]
+        arrived(w1b.at[:, pl.ds(0, 2), :, pl.ds(jo, size)], ag_sem.at[j, 1])
+
+    def near_sends(j, q):
+        return [
+            remote(w1_part(j, q), w1_part(j, q), send_sem.at[10 + j], ag_sem.at[j, 2], rows=near),
+            remote(w2_part(j, q), w2_part(j, q), send_sem.at[10 + j], ag_sem.at[j, 2], rows=near),
+        ]
+
+    def near_wait(j):
+        jo, size = p.blocks[j]
+        arrived(w1b.at[:, :, :, pl.ds(jo, size)], ag_sem.at[j, 2])
+
+    def start(copies):
+        for copy in copies:
+            copy.start()
+
+    def gather_one(j):
+        spread_wait(j)
+        start(far_sends(j))
+        start(near_sends(j, me_r))
+
+    def gather_two(j):
+        far_wait(j)
+        start(near_sends(j, far))
+
+    start(halo_sends())
+    for j in range(len(p.blocks)):
+        start(spread_sends(j))
+
+    loads[2].wait()
+    loads[3].wait()
+
+    gain = small_ref[8:9, :]
+    shift_row = small_ref[9:10, :]
+    scale = small_ref[14:15, :]
+
+    def forward_tile(b):
+        row = pl.multiple_of(b * TILE, TILE)
+        starts_here = flags[pl.ds(b, 1), :]
+        ends_here = flags[pl.ds(b + 1, 1), :]
+        lead = frx[pl.ds(row, HALO), :].astype(F32)
+        trail = frx[pl.ds(row + HALO + TILE, HALO), :].astype(F32)
+        for c in range(p.nc):
+            cols = slice(128 * c, 128 * c + 128)
+            xf[b, c, GAP : GAP + TILE, :] = frx[pl.ds(row + HALO, TILE), cols].astype(F32)
+            xf[b, c, 0:GAP, :] = jnp.where(starts_here > 0.5, 0.0, lead[HALO - GAP :, cols])
+            xf[b, c, GAP + TILE :, :] = jnp.where(ends_here > 0.5, 0.0, trail[0:GAP, cols])
+        for c in range(p.nc):
+            cols = slice(128 * c, 128 * c + 128)
+            total = jnp.broadcast_to(small_ref[7:8, cols], (TILE, 128))
+            for k in range(TAPS):
+                first = GAP - 3 + k
+                total = total + small_ref[k : k + 1, cols] * xf[b, c, first : first + TILE, :]
+            tmp[:, cols] = total
+        step = 32
+        for q in range(TILE // step):
+            rows = pl.ds(row + q * step, step)
+            value = tmp[q * step : q * step + step, :]
+            centred = value - jnp.sum(value, axis=1, keepdims=True) * (1.0 / p.d)
+            spread = jnp.sum(centred * centred, axis=1, keepdims=True) * (1.0 / p.d)
+            inverse = lax.rsqrt(spread + norm_eps)
+            unit = centred * inverse
+            rstd[rows, :] = jnp.broadcast_to(inverse, (step, 128))
+            xhat[rows, :] = unit.astype(BF16)
+            nm[rows, :] = (unit * gain + shift_row).astype(BF16)
+            low = (scale * ct[rows, :].astype(F32)).astype(BF16)
+            gb[rows, :] = low
+            accs[10] += fold(low.astype(F32))
+        nmt[:, pl.ds(row, TILE)] = nm[pl.ds(row, TILE), :].T
+        gbt[:, pl.ds(row, TILE)] = gb[pl.ds(row, TILE), :].T
+
+    def forward_tiles(low, high):
+        @pl.loop(low, high)
+        def _(b):
+            forward_tile(b)
+
+    nb = p.nb
+    cut = [1 + (nb - 2) * i // 4 for i in range(5)]
+    forward_tiles(cut[0], cut[1])
+    gather_one(0)
+    forward_tiles(cut[1], cut[2])
+    gather_two(0)
+    forward_tiles(cut[2], cut[3])
+    gather_one(1)
+    forward_tiles(cut[3], cut[4])
+    arrived(frx.at[pl.ds(0, HALO)], halo_sem.at[0])
+    arrived(frx.at[pl.ds(HALO + t_len, HALO)], halo_sem.at[1])
+
+    @pl.loop(0, 2)
+    def _(i):
+        forward_tile(i * (nb - 1))
+
+    near_wait(0)
+
+    def parts_of(j):
+        jo, size = p.blocks[j]
+        start_row, run = p.starts[j], p.runs[j]
+        return jo, size, start_row, run
+
+    def pair_sends(j):
+        jo, size, _, _ = parts_of(j)
+        out = []
+        for slot, q in ((0, near), (1, both)):
+            out.append(remote(s1w1.at[:, q, :, pl.ds(jo, size)], r1w1.at[slot, :, :, pl.ds(jo, size)], send_sem.at[14 + j], rs_sem.at[j, 0], rows=near))
+            out.append(remote(s1w2.at[q, pl.ds(jo, size), :], r1w2.at[slot, pl.ds(jo, size), :], send_sem.at[14 + j], rs_sem.at[j, 0], rows=near))
+        return out
+
+    def cross_sends(j):
+        jo, size, _, _ = parts_of(j)
+        return [
+            remote(s2w1.at[:, :, pl.ds(jo, size)], r2w1.at[:, :, pl.ds(jo, size)], send_sem.at[18 + j], rs_sem.at[j, 1], rows=far),
+            remote(s2w2.at[pl.ds(jo, size), :], r2w2.at[pl.ds(jo, size), :], send_sem.at[18 + j], rs_sem.at[j, 1], rows=far),
+        ]
+
+    def holder_sends(j):
+        jo, size, start_row, run = parts_of(j)
+        out = []
+        for step in range(1, nt):
+            peer = (me_t + step) % nt
+            out.append(remote(s3w1.at[peer, :, pl.ds(jo, size)], r3w1.at[me_t, :, pl.ds(jo, size)], send_sem.at[22 + j], rs_sem.at[j, 2], tm=peer))
+            out.append(remote(s3w2.at[pl.ds(pl.multiple_of(jo + run * peer, run), run), :], r3w2.at[me_t, pl.ds(start_row, run), :], send_sem.at[22 + j], rs_sem.at[j, 2], tm=peer))
+        return out
+
+    def final_sends(j):
+        jo, size, start_row, run = parts_of(j)
+        out = []
+        for step in range(1, nr):
+            peer = (me_r + step) % nr
+            one = finw1.at[me_r, :, pl.ds(jo, size)]
+            two = finw2.at[me_r, pl.ds(start_row, run), :]
+            out.append(remote(one, one, send_sem.at[26 + j], rs_sem.at[j, 3], rows=peer))
+            out.append(remote(two, two, send_sem.at[26 + j], rs_sem.at[j, 3], rows=peer))
+        return out
+
+    def sum_zero(j):
+        jo, size, _, _ = parts_of(j)
+        one = acc1[:, 0:size].astype(BF16).reshape(nt, nr, p.part, size)
+        s1w1[:, :, :, pl.ds(jo, size)] = one
+        two = acc2[:, 0:size].astype(BF16).T
+        for q in range(nr):
+            s1w2[q, pl.ds(jo, size), :] = two[:, p.lanes * q : p.lanes * q + p.lanes]
+        start(pair_sends(j))
+
+    def sum_one(j):
+        jo, size, _, _ = parts_of(j)
+        cols = pl.ds(jo, size)
+        arrived(s1w1.at[:, :, :, cols], rs_sem.at[j, 0])
+        one = s1w1[:, far, :, cols].astype(F32) + r1w1[1, :, :, cols].astype(F32)
+        s2w1[:, :, cols] = one.astype(BF16)
+        two = s1w2[far, cols, :].astype(F32) + r1w2[1, cols, :].astype(F32)
+        s2w2[cols, :] = two.astype(BF16)
+        start(cross_sends(j))
+
+    def sum_two(j):
+        jo, size, start_row, run = parts_of(j)
+        cols = pl.ds(jo, size)
+        arrived(s1w1.at[:, pl.ds(0, 2), :, cols], rs_sem.at[j, 1])
+        one = s1w1[:, me_r, :, cols].astype(F32) + r1w1[0, :, :, cols].astype(F32) + r2w1[:, :, cols].astype(F32)
+        s3w1[:, :, cols] = one.astype(BF16)
+        two = s1w2[me_r, cols, :].astype(F32) + r1w2[0, cols, :].astype(F32) + r2w2[cols, :].astype(F32)
+        s3w2[cols, :] = two.astype(BF16)
+        r3w1[me_t, :, cols] = s3w1[me_t, :, cols]
+        r3w2[me_t, pl.ds(start_row, run), :] = s3w2[pl.ds(pl.multiple_of(jo + run * me_t, run), run), :]
+        start(holder_sends(j))
+
+    def sum_three(j):
+        jo, size, start_row, run = parts_of(j)
+        cols = pl.ds(jo, size)
+        arrived(s1w1.at[pl.ds(0, nt - 1), pl.ds(0, 2), :, cols], rs_sem.at[j, 2])
+        one = r3w1[0, :, cols].astype(F32)
+        two = r3w2[0, pl.ds(start_row, run), :].astype(F32)
+        for k in range(1, nt):
+            one = one + r3w1[k, :, cols].astype(F32)
+            two = two + r3w2[k, pl.ds(start_row, run), :].astype(F32)
+        finw1[me_r, :, cols] = one
+        finw2[me_r, pl.ds(start_row, run), :] = two
+        start(final_sends(j))
+
+    def sum_wait(j):
+        jo, size, _, _ = parts_of(j)
+        arrived(s1w1.at[pl.ds(0, 3 * nt // 4), pl.ds(0, 2), :, pl.ds(jo, size)], rs_sem.at[j, 3])
+
+    m = p.m
+    per = m // TILE
+
+    def rows_add(ref, i, value, first):
+        for s in range(per):
+            for c in range(p.nc):
+                piece = value[TILE * s : TILE * s + TILE, 128 * c : 128 * c + 128]
+                place = (i * per + s, c, slice(GAP, GAP + TILE), slice(None))
+                ref[place] = piece if first else ref[place] + piece
+
+    def main_block(j, between):
+        jo, size = p.blocks[j]
+        cols = pl.ds(jo, size)
+        acc1[:, 0:size] = jnp.zeros((p.d, size), F32)
+        acc2[:, 0:size] = jnp.zeros((p.d, size), F32)
+
+        @pl.loop(0, t_len // m)
+        def _(i):
+            for at, task in between:
+                pl.when(i == at)(task)
+            rows = pl.ds(pl.multiple_of(i * m, m), m)
+            w1 = w1b[:, :, :, cols].reshape(p.d, size)
+            w2 = jnp.concatenate([w2b[q, cols, :] for q in range(nr)], axis=1)
+            hidden = jnp.dot(nm[rows, :], w1, preferred_element_type=F32) + b1p[0:1, cols]
+            grad_act = lax.dot_general(
+                gb[rows, :], w2, (((1,), (1,)), ((), ())), preferred_element_type=F32
+            )
+            prob = 0.5 * (1.0 + lax.erf(hidden * RSQRT_HALF))
+            bell = jnp.exp(hidden * hidden * np.float32(-0.5)) * RSQRT_2PI
+            act = (hidden * prob).astype(BF16)
+            grad_hidden = (grad_act * (prob + hidden * bell)).astype(BF16)
+            accb[:, cols] += fold(grad_hidden.astype(F32))
+            rows_add(br, i, jnp.dot(act, w2, preferred_element_type=F32), j == 0)
+            back = lax.dot_general(
+                grad_hidden, w1, (((1,), (1,)), ((), ())), preferred_element_type=F32
+            )
+            gn[rows, :] = back if j == 0 else gn[rows, :] + back
+            acc1[:, 0:size] += jnp.dot(nmt[:, rows], grad_hidden, preferred_element_type=F32)
+            acc2[:, 0:size] += jnp.dot(gbt[:, rows], act, preferred_element_type=F32)
+
+    main_block(0, [(1, lambda: gather_two(1)), (2, lambda: gather_one(2))])
+    sum_zero(0)
+    near_wait(1)
+    main_block(
+        1, [(0, lambda: gather_two(2)), (1, lambda: sum_one(0)), (1, lambda: gather_one(3)), (2, lambda: sum_two(0)), (2, lambda: gather_two(3))]
+    )
+    sum_zero(1)
+    near_wait(2)
+    main_block(2, [(0, lambda: sum_three(0)), (1, lambda: sum_one(1))])
+    sum_zero(2)
+    sum_two(1)
+    near_wait(3)
+    main_block(3, [(1, lambda: sum_one(2)), (2, lambda: sum_three(1))])
+    sum_zero(3)
+    sum_two(2)
+
+    def output_copy(b):
+        rows = pl.ds(pl.multiple_of(b * TILE, TILE), TILE)
+        return pltpu.make_async_copy(nm.at[rows], output_hbm.at[0, rows], out_sem.at[0])
+
+    def ingrad_copy(b):
+        rows = pl.ds(pl.multiple_of(b * TILE, TILE), TILE)
+        return pltpu.make_async_copy(gb.at[rows], ingrad_hbm.at[0, rows], out_sem.at[1])
+
+    bias_two = small_ref[13:14, :]
+
+    def backward_tile(b):
+        row = pl.multiple_of(b * TILE, TILE)
+        step = 32
+        for q in range(TILE // step):
+            rows = pl.ds(row + q * step, step)
+            place = slice(GAP + q * step, GAP + q * step + step)
+            branch = jnp.concatenate([br[b, c, place, :] for c in range(p.nc)], axis=1) + bias_two
+            source = frx[pl.ds(row + HALO + q * step, step), :].astype(F32)
+            nm[rows, :] = (source + scale * branch).astype(BF16)
+            accs[11] += fold(ct[rows, :].astype(F32) * branch)
+            grad = gn[rows, :]
+            unit = xhat[rows, :].astype(F32)
+            accs[8] += fold(grad * unit)
+            accs[9] += fold(grad)
+            u = grad * gain
+            mean_u = jnp.sum(u, axis=1, keepdims=True) * (1.0 / p.d)
+            mean_x = jnp.sum(u * unit, axis=1, keepdims=True) * (1.0 / p.d)
+            inverse = rstd[rows, :]
+            inverse = jnp.concatenate([inverse] * p.nc, axis=1)
+            low = ((u - mean_u - unit * mean_x) * inverse).astype(BF16).astype(F32)
+            accs[7] += fold(low)
+            for c in range(p.nc):
+                br[b, c, place, :] = low[:, 128 * c : 128 * c + 128]
+        for c in range(p.nc):
+            cols = slice(128 * c, 128 * c + 128)
+            low = br[b, c, GAP : GAP + TILE, :]
+            for k in range(TAPS):
+                first = GAP - 3 + k
+                accs[k, :, cols] += fold(low * xf[b, c, first : first + TILE, :])
+        output_copy(b).start()
+
+    def backward_tiles(low, high):
+        @pl.loop(low, high)
+        def _(b):
+            backward_tile(b)
+
+    def edge_sends():
+        after, before = (me_t + 1) % nt, (me_t + nt - 1) % nt
+        return [
+            remote(br.at[nb - 1, :, pl.ds(TILE, GAP), :], hprev, send_sem.at[30], halo_sem.at[2], tm=after),
+            remote(br.at[0, :, pl.ds(GAP, GAP), :], hnext, send_sem.at[31], halo_sem.at[3], tm=before),
+        ]
+
+    @pl.loop(0, 2)
+    def _(i):
+        backward_tile(i * (nb - 1))
+
+    start(edge_sends())
+    sum_one(3)
+    cut = [1 + (nb - 2) * i // 4 for i in range(5)]
+    backward_tiles(cut[0], cut[1])
+    sum_three(2)
+    backward_tiles(cut[1], cut[2])
+    sum_two(3)
+    backward_tiles(cut[2], cut[4])
+    sum_three(3)
+
+    hidden_tiles = lane_permuted(lambda i: accb[:, 128 * i : 128 * i + 128], p.regrouped, p.ff // 128)
+    for c in range(p.nc):
+        cols = slice(128 * c, 128 * c + 128)
+        line = []
+        for k in range(10):
+            line.append(jnp.sum(accs[k, :, cols], axis=0, keepdims=True))
+        for i in range(3):
+            line.append(jnp.sum(hidden_tiles[i * p.nc + c], axis=0, keepdims=True))
+        for k in (10, 11):
+            line.append(jnp.sum(accs[k, :, cols], axis=0, keepdims=True))
+        line.append(jnp.zeros((1, 128), F32))
+        sma[c] = jnp.concatenate(line, axis=0)
+
+    def small_one_sends():
+        out = []
+        for step in range(1, nr):
+            peer = (me_r + step) % nr
+            out.append(remote(sma.at[peer], smr.at[me_r], send_sem.at[32], sm_sem.at[0], rows=peer))
+        return out
+
+    def small_two_sends():
+        out = []
+        for step in range(1, nt):
+            peer = (me_t + step) % nt
+            out.append(remote(smq.at[nt], smq.at[me_t], send_sem.at[33], sm_sem.at[1], tm=peer))
+        return out
+
+    def small_three_sends():
+        out = []
+        for step in range(1, nr):
+            peer = (me_r + step) % nr
+            out.append(remote(smf.at[me_r], smf.at[me_r], send_sem.at[34], sm_sem.at[2], rows=peer))
+        return out
+
+    smr[me_r] = sma[me_r]
+    start(small_one_sends())
+
+    def small_two():
+        arrived(smr.at[pl.ds(0, nr - 1)], sm_sem.at[0])
+        total = smr[0]
+        for k in range(1, nr):
+            total = total + smr[k]
+        smq[nt] = total
+        smq[me_t] = total
+        start(small_two_sends())
+
+    def small_three():
+        arrived(smq.at[pl.ds(0, nt - 1)], sm_sem.at[1])
+        total = smq[0]
+        for k in range(1, nt):
+            total = total + smq[k]
+        smf[me_r] = total
+        start(small_three_sends())
+
+    def exchange_edges(b):
+        same = flags[pl.ds(b, 1), :] < 0.5
+        for c in range(p.nc):
+            br[b, c, 0:GAP, :] = jnp.where(same, br[b - 1, c, TILE : TILE + GAP, :], 0.0)
+            br[b - 1, c, GAP + TILE :, :] = jnp.where(same, br[b, c, GAP : GAP + GAP, :], 0.0)
+
+    def input_tile(b):
+        row = pl.multiple_of(b * TILE, TILE)
+        for c in range(p.nc):
+            cols = slice(128 * c, 128 * c + 128)
+            total = ct[pl.ds(row, TILE), cols].astype(F32)
+            for k in range(TAPS):
+                first = GAP + 3 - k
+                total = total + small_ref[k : k + 1, cols] * br[b, c, first : first + TILE, :]
+            gb[pl.ds(row, TILE), cols] = total.astype(BF16)
+        ingrad_copy(b).start()
+
+    exchange_edges(1)
+
+    def input_tiles(low, high):
+        @pl.loop(low, high)
+        def _(b):
+            exchange_edges(b + 1)
+            input_tile(b)
+
+    cut = [1 + (nb - 2) * i // 4 for i in range(5)]
+    input_tiles(cut[0], cut[1])
+    small_two()
+    input_tiles(cut[1], cut[3])
+    small_three()
+    input_tiles(cut[3], cut[4])
+    arrived(hprev, halo_sem.at[2])
+    arrived(hnext, halo_sem.at[3])
+    for c in range(p.nc):
+        br[0, c, 0:GAP, :] = jnp.where(flags[0:1, :] < 0.5, hprev[c], 0.0)
+        br[nb - 1, c, GAP + TILE :, :] = jnp.where(flags[nb : nb + 1, :] < 0.5, hnext[c], 0.0)
+
+    @pl.loop(0, 2)
+    def _(i):
+        input_tile(i * (nb - 1))
+
+    for j in range(len(p.blocks)):
+        sum_wait(j)
+    for q in range(nr):
+        tiles = lane_permuted(lambda i, q=q: finw1[q, :, 128 * i : 128 * i + 128], p.regrouped, p.ff // 128)
+        for i, tile in enumerate(tiles):
+            g1_out[p.part * q : p.part * q + p.part, 128 * i : 128 * i + 128] = tile
+        g2_out[:, p.lanes * q : p.lanes * q + p.lanes] = finw2[q]
+    arrived(smf.at[pl.ds(0, nr - 1)], sm_sem.at[2])
+    for c in range(p.nc):
+        small_out[:, 128 * c : 128 * c + 128] = smf[c]
+
+    sent = halo_sends() + edge_sends() + small_one_sends() + small_two_sends() + small_three_sends()
+    for j in range(len(p.blocks)):
+        sent += spread_sends(j) + far_sends(j) + near_sends(j, me_r) + near_sends(j, far)
+        sent += pair_sends(j) + cross_sends(j) + holder_sends(j) + final_sends(j)
+    for copy in sent:
+        copy.wait_send()
+    whole = pl.ds(0, t_len)
+    pltpu.make_async_copy(nm.at[whole], output_hbm.at[0, whole], out_sem.at[0]).wait()
+    pltpu.make_async_copy(gb.at[whole], ingrad_hbm.at[0, whole], out_sem.at[1]).wait()
+
+
+def call(plan, frames, cotangent, lengths, w1_master, w2_master, small_master):
+    p = plan
+    t, d, ff, nt, nr, nb, nc = p.t, p.d, p.ff, p.nt, p.nr, p.nb, p.nc
+    vmem = pl.BlockSpec(memory_space=pltpu.VMEM)
+    anyplace = pl.BlockSpec(memory_space=pl.ANY)
+    n_lens = -(-lengths.shape[1] // 128) * 128
+    v = pltpu.VMEM
+    scratch = [
+        v((t + 2 * HALO, d), BF16),
+        v((t, d), BF16),
+        v((t, d), BF16),
+        v((d, t), BF16),
+        v((t, d), BF16),
+        v((d, t), BF16),
+        v((nb, nc, TILE + 2 * GAP, 128), F32),
+        v((t, d), F32),
+        v((nb, nc, TILE + 2 * GAP, 128), F32),
+        v((t, d), BF16),
+        v((t, 128), F32),
+        v((nt, nr, p.part, ff), BF16),
+        v((nr, ff, p.lanes), BF16),
+        v((p.part, ff), F32),
+        v((p.share, p.lanes), F32),
+        v((d, p.widest), F32),
+        v((d, p.widest), F32),
+        v((8, n_lens), F32),
+        v((-(-(nb + 1) // 8) * 8, 128), F32),
+        v((8, ff), F32),
+        v((12, 8, d), F32),
+        v((8, ff), F32),
+        v((TILE, d), F32),
+        v((nt, nr, p.part, ff), BF16),
+        v((nr, ff, p.lanes), BF16),
+        v((2, nt, p.part, ff), BF16),
+        v((2, ff, p.lanes), BF16),
+        v((nt, p.part, ff), BF16),
+        v((ff, p.lanes), BF16),
+        v((nt, p.part, ff), BF16),
+        v((ff, p.lanes), BF16),
+        v((nt, p.part, ff), BF16),
+        v((ff, p.lanes), BF16),
+        v((nt, p.part, ff), BF16),
+        v((nt, p.share, p.lanes), BF16),
+        v((nr, p.part, ff), F32),
+        v((nr, p.share, p.lanes), F32),
+        v((nr, 16, p.lanes), F32),
+        v((nr, 16, p.lanes), F32),
+        v((nt + 1, 16, p.lanes), F32),
+        v((nr, 16, p.lanes), F32),
+        v((nc, GAP, 128), F32),
+        v((nc, GAP, 128), F32),
+        pltpu.SemaphoreType.DMA((4,)),
+        pltpu.SemaphoreType.DMA((2,)),
+        pltpu.SemaphoreType.DMA((35,)),
+        pltpu.SemaphoreType.DMA((4,)),
+        pltpu.SemaphoreType.DMA((4, 3)),
+        pltpu.SemaphoreType.DMA((4, 4)),
+        pltpu.SemaphoreType.DMA((3,)),
+    ]
+    return pl.pallas_call(
+        functools.partial(kernel, plan),
+        out_shape=(
+            jax.ShapeDtypeStruct((1, t, d), BF16),
+            jax.ShapeDtypeStruct((1, t, d), BF16),
+            jax.ShapeDtypeStruct((p.rows1, ff), F32),
+            jax.ShapeDtypeStruct((p.share, d), F32),
+            jax.ShapeDtypeStruct((16, d), F32),
+        ),
+        in_specs=[anyplace, anyplace, vmem, anyplace, anyplace, vmem],
+        out_specs=(anyplace, anyplace, vmem, vmem, vmem),
+        scratch_shapes=scratch,
+        compiler_params=pltpu.CompilerParams(
+            collective_id=0, has_side_effects=True, vmem_limit_bytes=67_000_000
+        ),
+    )(frames, cotangent, lengths, w1_master, w2_master, small_master)
 
 
 def padded_2(array, sides, width):
@@ -72,25 +825,13 @@
     return jax.nn.gelu(values, approximate=False)
 
 
-def adamw_step(master, first_old, second_old, average_old, gradient, rate):
-    first_new = beta_first * first_old + (1.0 - beta_first) * gradient
-    second_new = beta_second * second_old + (1.0 - beta_second) * gradient * gradient
-    first_hat = first_new / (1.0 - beta_first**ADAM_STEP)
-    second_hat = second_new / (1.0 - beta_second**ADAM_STEP)
-    master_new = master - rate * (
-        first_hat / (jnp.sqrt(second_hat) + adam_eps) + weight_decay * master
-    )
-    average_new = average_keep * average_old + (1.0 - average_keep) * master_new
-    return (master_new, first_new, second_new, average_new, master_new.astype(jnp.bfloat16))
-
-
 def frame_product(left_side, right_side):
     return lax.dot_general(
         left_side, right_side, (((0,), (0,)), ((), ())), preferred_element_type=jnp.float32
     )
 
 
-def body(
+def plain_body(
     frames,
     cotangent,
     lengths,
@@ -200,6 +941,36 @@
     )
 
 
+def body(
+    frames,
+    cotangent,
+    lengths,
+    w1_master,
+    w1_first,
+    w1_second,
+    w1_average,
+    w2_master,
+    w2_first,
+    w2_second,
+    w2_average,
+    small_master,
+    small_first,
+    small_second,
+    small_average,
+):
+    nt, nr = lax.axis_size("tm"), lax.axis_size("rows")
+    plan = Plan(nt, nr, frames.shape[1], frames.shape[2], w1_master.shape[1])
+    output, input_grad, grad_one, grad_two, small_total = call(
+        plan, frames, cotangent, lengths, w1_master, w2_master, small_master
+    )
+    one_out = adamw_step(w1_master, w1_first, w1_second, w1_average, grad_one, rate_first)
+    two_out = adamw_step(w2_master, w2_first, w2_second, w2_average, grad_two, rate_second)
+    small_out = adamw_step(
+        small_master, small_first, small_second, small_average, small_total[:15], rate_small
+    )
+    return (output, input_grad, *one_out, *two_out, *small_out)
+
+
 def solution(mesh):
     in_specs = (
         P("rows", "tm", None),
@@ -237,4 +1008,5 @@
         P(),
         P(),
     )
-    return jax.shard_map(body, mesh=mesh, in_specs=in_specs, out_specs=out_specs, check_vma=False)
+    fits = mesh.shape["tm"] == 8 and mesh.shape["rows"] == 4
+    return jax.shard_map(body if fits else plain_body, mesh=mesh, in_specs=in_specs, out_specs=out_specs, check_vma=False)

time: 311 us -> 109 us (0.35)
  matrix products: 108 us -> 0 us
  Pallas kernels: 0 us -> 96.4 us
  other arithmetic: 82.7 us -> 6.73 us
  blocking collectives: 41 us -> 0 us
  waiting for transfers between devices: 34.4 us -> 0 us
  starting transfers between devices: 20.6 us -> 0 us
  between operations: 14.5 us -> 0.77 us
  local copies, waits for them, and re-layouts: 8.58 us -> 4.76 us
    dot_general x6 -> x0, matrix products: 108 us -> none  [the longest x1 49.9 us: body(): jnp.dot(normed_low, w1_low, preferred_element_type=jnp.float32)]
    pallas_call x0 -> x1, Pallas kernels: none -> 96.4 us  [call(): pl.pallas_call(functools.partial(kernel, plan), out_shape=(jax.ShapeDtype...]
    reduce_sum x7 -> x0, other arithmetic: 53.9 us -> none  [the longest x2 24.2 us: layer_norm(): centred = conv_out - jnp.mean(conv_out, axis=-1, keepdims=True)]
    psum x1 -> x0, blocking collectives: 41 us -> none  [body(): small_total = lax.psum(small_grad, ('tm', 'rows'))]
    psum x1 -> x0, waiting for transfers between devices: 18.2 us -> none  [body(): lax.psum(share_one.astype(jnp.bfloat16), 'rows').astype(jnp.float32)]
    broadcast_in_dim x1 -> x0, other arithmetic: 15.3 us -> none  [body(): input_grad[None]]
    ppermute x4 -> x0, starting transfers between devices: 11.7 us -> none  [the longest x2 9.14 us: padded_2(): before = lax.ppermute(last, axis, up)]
    all_gather x2 -> x0, waiting for transfers between devices: 10.5 us -> none  [the longest x1 10.5 us: body(): lax.all_gather(w1_master.astype(jnp.bfloat16), 'tm', axis=0, tiled=True)]
  transfers between devices with their start and end apart: 9 -> 0, of which waited for: 3 -> 0; matrix products, arithmetic and copies ran while one was open for 50% -> 0% of each run, Pallas kernels for 0% -> 0%
where the time goes in v1:
time: 109 us
  Pallas kernels  96.4 us (88%)
  other arithmetic  6.73 us (6%)
  local copies, waits for them, and re-layouts  4.76 us (4%)
    pallas_call x1, Pallas kernels, call(): pl.pallas_call(functools.partial(kernel, plan), out_shape=(jax.ShapeDtype...  96.4 us
    unnamed x34, local copies, waits for them, and re-layouts  4.76 us
    convert_element_type x3, other arithmetic, adamw_step(): master_new.astype(BF16)  4.44 us
    add x3, other arithmetic, adamw_step(): average_new = average_keep * average_old + (1.0 - average_keep) * master_new  2.29 us

profile of v1, /device:TPU:0, one launch (start us, length us, event | category | flops | bytes accessed | tf_op | source)
XLA Modules:
  0.0 108.7 jit_solution(4236496673475272218)
XLA Ops:
  0.7 96.4 %shard_map.278 = (bf16[1,3072,512]{2,1,0:T(8,128)(2,1)}, bf16[1,3072,512]{2,1,0:T(8,128)(2,1)}, f32[64,1536]{1,0:T(8,128)}, f32[192,512]{1,0:T(8,128)}, f32[16,512]{1,0:T(8,128)}) custom-call(bf16[1,3072,512]{2,1,0:T(8,128)(2,1)} %frames_hbm.1, bf16[1,3072,512]{2,1,0:T(8,128)(2,1)} %cot_hbm.1, s32[1,80]{1,0:T(1,128)} %lengths_ref.1, f32[64,1536]{1,0:T(8,128)} %w1_hbm.1, ...), custom_call_target="tpu_custom_call" | custom-call | tf_op jit(solution)/shard_map/pallas_call | solution.py:755
  97.1 0.0 copy-start.5
  97.1 0.0 copy-start.2
  97.1 0.0 copy-start.7
  97.1 0.0 copy-start.8
  97.1 0.0 copy-start.9
  97.2 0.0 copy-start.6
  97.2 2.6 %fusion.7 = (bf16[64,1536]{1,0:T(8,128)(2,1)}, f32[64,1536]{1,0:T(8,128)S(1)}, f32[64,1536]{1,0:T(8,128)}, f32[64,1536]{1,0:T(8,128)}) fusion(f32[64,1536]{1,0:T(8,128)} %w1_hbm.1, f32[64,1536]{1,0:T(8,128)} %get-tuple-element.24, f32[64,1536]{1,0:T(8,128)} %param.19, f32[64,1536]{1,0:T(8,128)} %param.20), kind=kLoop, calls=%fused_computation.17 | loop fusion | flops 1474560 | bytes 2949120 | tf_op jit(solution)/shard_map/convert_element_type | solution.py:43
  99.8 0.0 copy-start.13
  99.8 0.0 copy-start.15
  99.8 0.0 copy-start.14
  99.9 0.0 copy-start.1
  99.9 0.0 copy-done.5
  99.9 0.8 multiply_add_fusion.3
  100.7 0.0 copy-done.2
  100.7 1.2 %fusion.5 = (bf16[192,512]{1,0:T(8,128)(2,1)}, f32[192,512]{1,0:T(8,128)S(1)}, f32[192,512]{1,0:T(8,128)}, f32[192,512]{1,0:T(8,128)}) fusion(f32[192,512]{1,0:T(8,128)S(1)} %copy-done.2, f32[192,512]{1,0:T(8,128)S(1)} %copy-done.9, f32[192,512]{1,0:T(8,128)S(1)} %copy-done.7, f32[192,512]{1,0:T(8,128)S(1)} %copy-done.8), kind=kLoop, calls=%fused_computation.16 | loop fusion | flops 1474560 | bytes 2949120 | tf_op jit(solution)/shard_map/convert_element_type | solution.py:43
  101.8 0.9 multiply_add_fusion.2
  102.7 0.0 copy-done.13
  102.7 0.6 fusion.3
  103.4 0.6 multiply_add_fusion.5
  104.0 1.7 %copy.34 = bf16[1,3072,512]{2,1,0:T(8,128)(2,1)} copy(bf16[1,3072,512]{2,1,0:T(8,128)(2,1)S(1)} %copy-done.1) | data formatting | bytes 6291456
  105.7 0.0 copy-done.4
  105.7 1.4 %copy-done = bf16[1,3072,512]{2,1,0:T(8,128)(2,1)S(1)} copy-done((bf16[1,3072,512]{2,1,0:T(8,128)(2,1)S(1)}, bf16[1,3072,512]{2,1,0:T(8,128)(2,1)}, u32[]{:S(2)}) %copy-start) | copy-done | bytes 3145752
  107.0 1.7 %copy.35 = bf16[1,3072,512]{2,1,0:T(8,128)(2,1)} copy(bf16[1,3072,512]{2,1,0:T(8,128)(2,1)S(1)} %copy-done) | data formatting | bytes 6291456
  (17 shorter events, 0.0 us)
Async XLA Ops:
  97.1 2.8 %copy-start.5 = (f32[64,1536]{1,0:T(8,128)S(1)}, f32[64,1536]{1,0:T(8,128)}, u32[]{:S(2)}) copy-start(f32[64,1536]{1,0:T(8,128)} %param.21) | copy-start | bytes 1179652
  97.1 3.6 %copy-start.2 = (f32[192,512]{1,0:T(8,128)S(1)}, f32[192,512]{1,0:T(8,128)}, u32[]{:S(2)}) copy-start(f32[192,512]{1,0:T(8,128)} %w2_hbm.1) | copy-start | bytes 1179652
  97.1 3.6 %copy-start.7 = (f32[192,512]{1,0:T(8,128)S(1)}, f32[192,512]{1,0:T(8,128)}, u32[]{:S(2)}) copy-start(f32[192,512]{1,0:T(8,128)} %param.23) | copy-start | bytes 1179652
  97.1 3.5 %copy-start.8 = (f32[192,512]{1,0:T(8,128)S(1)}, f32[192,512]{1,0:T(8,128)}, u32[]{:S(2)}) copy-start(f32[192,512]{1,0:T(8,128)} %param.24) | copy-start | bytes 1179652
  97.1 3.5 %copy-start.9 = (f32[192,512]{1,0:T(8,128)S(1)}, f32[192,512]{1,0:T(8,128)}, u32[]{:S(2)}) copy-start(f32[192,512]{1,0:T(8,128)} %get-tuple-element.25) | copy-start | bytes 1179652
  97.2 4.7 %copy-start.6 = (f32[192,512]{1,0:T(8,128)S(1)}, f32[192,512]{1,0:T(8,128)}, u32[]{:S(2)}) copy-start(f32[192,512]{1,0:T(8,128)} %param.25) | copy-start | bytes 1179652
  99.8 5.9 %copy-start.3 = (f32[64,1536]{1,0:T(8,128)}, f32[64,1536]{1,0:T(8,128)S(1)}, u32[]{:S(2)}) copy-start(f32[64,1536]{1,0:T(8,128)S(1)} %get-tuple-element.58) | copy-start | bytes 1179652
  99.8 2.9 %copy-start.10 = (f32[15,512]{1,0:T(8,128)S(1)}, f32[15,512]{1,0:T(8,128)}, u32[]{:S(2)}) copy-start(f32[15,512]{1,0:T(8,128)} %small_ref.1) | copy-start | bytes 92164
  99.8 2.9 %copy-start.12 = (f32[15,512]{1,0:T(8,128)S(1)}, f32[15,512]{1,0:T(8,128)}, u32[]{:S(2)}) copy-start(f32[15,512]{1,0:T(8,128)} %param.27) | copy-start | bytes 92164
  99.8 2.9 %copy-start.13 = (f32[15,512]{1,0:T(8,128)S(1)}, f32[15,512]{1,0:T(8,128)}, u32[]{:S(2)}) copy-start(f32[15,512]{1,0:T(8,128)} %param.28) | copy-start | bytes 92164
  99.8 2.9 %copy-start.15 = (f32[16,512]{1,0:T(8,128)S(1)}, f32[16,512]{1,0:T(8,128)}, u32[]{:S(2)}) copy-start(f32[16,512]{1,0:T(8,128)} %get-tuple-element.26) | copy-start | bytes 98308
  99.8 3.5 %copy-start.14 = (f32[15,512]{1,0:T(8,128)S(1)}, f32[15,512]{1,0:T(8,128)}, u32[]{:S(2)}) copy-start(f32[15,512]{1,0:T(8,128)} %param.29) | copy-start | bytes 92164
  99.9 4.2 %copy-start.1 = (bf16[1,3072,512]{2,1,0:T(8,128)(2,1)S(1)}, bf16[1,3072,512]{2,1,0:T(8,128)(2,1)}, u32[]{:S(2)}) copy-start(bf16[1,3072,512]{2,1,0:T(8,128)(2,1)} %get-tuple-element.56) | copy-start | bytes 9437188
  101.8 3.8 %copy-start.4 = (f32[192,512]{1,0:T(8,128)}, f32[192,512]{1,0:T(8,128)S(1)}, u32[]{:S(2)}) copy-start(f32[192,512]{1,0:T(8,128)S(1)} %get-tuple-element.63) | copy-start | bytes 1179652
  103.4 2.3 %copy-start.11 = (f32[15,512]{1,0:T(8,128)}, f32[15,512]{1,0:T(8,128)S(1)}, u32[]{:S(2)}) copy-start(f32[15,512]{1,0:T(8,128)S(1)} %get-tuple-element.68) | copy-start | bytes 92164
  104.0 3.0 %copy-start = (bf16[1,3072,512]{2,1,0:T(8,128)(2,1)S(1)}, bf16[1,3072,512]{2,1,0:T(8,128)(2,1)}, u32[]{:S(2)}) copy-start(bf16[1,3072,512]{2,1,0:T(8,128)(2,1)} %get-tuple-element.57) | copy-start | bytes 9437188

commit v2 on v1

--- a/solution.py
+++ b/solution.py
@@ -52,8 +52,8 @@
         self.lanes = width // nr
         self.nb = frame_count // TILE
         self.nc = width // 128
-        self.runs = [32, 64, 64, 32]
-        self.starts = [0, 32, 96, 160]
+        self.runs = [32, 32, 64, 32, 32]
+        self.starts = [0, 32, 64, 128, 160]
         self.blocks = []
         offset = 0
         for run in self.runs:
@@ -103,18 +103,24 @@
     cot_hbm,
     lengths_ref,
     w1_hbm,
+    w1_first_hbm,
+    w1_second_hbm,
+    w1_average_hbm,
     w2_hbm,
+    w2_first_hbm,
+    w2_second_hbm,
+    w2_average_hbm,
     small_ref,
-    output_hbm,
-    ingrad_hbm,
+    nm,
+    gb,
     g1_out,
     g2_out,
     small_out,
+    state1,
+    state2,
     frx,
     ct,
-    nm,
     nmt,
-    gb,
     gbt,
     br,
     gn,
@@ -123,8 +129,6 @@
     rstd,
     w1b,
     w2b,
-    m1,
-    m2,
     acc1,
     acc2,
     lens,
@@ -137,12 +141,8 @@
     s1w2,
     r1w1,
     r1w2,
-    s2w1,
-    s2w2,
     r2w1,
     r2w2,
-    s3w1,
-    s3w2,
     r3w1,
     r3w2,
     finw1,
@@ -154,7 +154,6 @@
     hprev,
     hnext,
     in_sem,
-    out_sem,
     send_sem,
     halo_sem,
     ag_sem,
@@ -180,8 +179,8 @@
         pltpu.make_async_copy(view, view, sem).wait()
 
     loads = [
-        pltpu.make_async_copy(w1_hbm.at[pl.ds(pl.multiple_of(me_r * p.part, p.part), p.part)], m1, in_sem.at[0]),
-        pltpu.make_async_copy(w2_hbm.at[:, pl.ds(pl.multiple_of(me_r * p.lanes, p.lanes), p.lanes)], m2, in_sem.at[1]),
+        pltpu.make_async_copy(w1_hbm, state1.at[0], in_sem.at[0]),
+        pltpu.make_async_copy(w2_hbm, state2.at[0], in_sem.at[1]),
         pltpu.make_async_copy(frames_hbm.at[0], frx.at[pl.ds(HALO, t_len)], in_sem.at[2]),
         pltpu.make_async_copy(cot_hbm.at[0], ct, in_sem.at[3]),
     ]
@@ -224,19 +223,21 @@
 
     loads[0].wait()
     loads[1].wait()
-    own1 = lane_permuted(lambda i: m1[:, 128 * i : 128 * i + 128], p.natural, p.ff // 128)
+    own_rows = pl.ds(pl.multiple_of(me_r * p.part, p.part), p.part)
+    own_lanes = pl.ds(pl.multiple_of(me_r * p.lanes, p.lanes), p.lanes)
+    own1 = lane_permuted(lambda i: state1[0, own_rows, 128 * i : 128 * i + 128], p.natural, p.ff // 128)
     for i, tile in enumerate(own1):
         w1b[me_t, me_r, :, 128 * i : 128 * i + 128] = tile.astype(BF16)
     for (jo, _), run, start in zip(p.blocks, p.runs, p.starts):
-        w2b[me_r, pl.ds(pl.multiple_of(jo + run * me_t, run), run), :] = m2[start : start + run, :].astype(BF16)
+        w2b[me_r, pl.ds(pl.multiple_of(jo + run * me_t, run), run), :] = state2[0, start : start + run, own_lanes].astype(BF16)
 
     pl.semaphore_wait(barrier, nt + nr - 2)
 
     def halo_sends():
         after, before = (me_t + 1) % nt, (me_t + nt - 1) % nt
         return [
-            remote(frames_hbm.at[0, pl.ds(t_len - HALO, HALO)], frx.at[pl.ds(0, HALO)], send_sem.at[0], halo_sem.at[0], tm=after),
-            remote(frames_hbm.at[0, pl.ds(0, HALO)], frx.at[pl.ds(HALO + t_len, HALO)], send_sem.at[1], halo_sem.at[1], tm=before),
+            remote(frames_hbm.at[0, pl.ds(t_len - HALO, HALO)], frx.at[pl.ds(0, HALO)], send_sem.at[7, 0], halo_sem.at[0], tm=after),
+            remote(frames_hbm.at[0, pl.ds(0, HALO)], frx.at[pl.ds(HALO + t_len, HALO)], send_sem.at[7, 1], halo_sem.at[1], tm=before),
         ]
 
     def w1_part(j, q):
@@ -255,8 +256,8 @@
             peer = (me_t + step) % nt
             one = w1b.at[me_t, me_r, :, pl.ds(jo, size)]
             two = w2b.at[me_r, pl.ds(pl.multiple_of(jo + run * me_t, run), run), :]
-            out.append(remote(one, one, send_sem.at[2 + j], ag_sem.at[j, 0], tm=peer))
-            out.append(remote(two, two, send_sem.at[2 + j], ag_sem.at[j, 0], tm=peer))
+            out.append(remote(one, one, send_sem.at[0, j], ag_sem.at[j, 0], tm=peer))
+            out.append(remote(two, two, send_sem.at[0, j], ag_sem.at[j, 0], tm=peer))
         return out
 
     def spread_wait(j):
@@ -265,8 +266,8 @@
 
     def far_sends(j):
         return [
-            remote(w1_part(j, me_r), w1_part(j, me_r), send_sem.at[6 + j], ag_sem.at[j, 1], rows=far),
-            remote(w2_part(j, me_r), w2_part(j, me_r), send_sem.at[6 + j], ag_sem.at[j, 1], rows=far),
+            remote(w1_part(j, me_r), w1_part(j, me_r), send_sem.at[1, j], ag_sem.at[j, 1], rows=far),
+            remote(w2_part(j, me_r), w2_part(j, me_r), send_sem.at[1, j], ag_sem.at[j, 1], rows=far),
         ]
 
     def far_wait(j):
@@ -275,8 +276,8 @@
 
     def near_sends(j, q):
         return [
-            remote(w1_part(j, q), w1_part(j, q), send_sem.at[10 + j], ag_sem.at[j, 2], rows=near),
-            remote(w2_part(j, q), w2_part(j, q), send_sem.at[10 + j], ag_sem.at[j, 2], rows=near),
+            remote(w1_part(j, q), w1_part(j, q), send_sem.at[2, j], ag_sem.at[j, 2], rows=near),
+            remote(w2_part(j, q), w2_part(j, q), send_sem.at[2, j], ag_sem.at[j, 2], rows=near),
         ]
 
     def near_wait(j):
@@ -300,6 +301,19 @@
     for j in range(len(p.blocks)):
         start(spread_sends(j))
 
+    rest = [
+        pltpu.make_async_copy(source, target, in_sem.at[4])
+        for source, target in (
+            (w1_first_hbm, state1.at[1]),
+            (w1_second_hbm, state1.at[2]),
+            (w1_average_hbm, state1.at[3]),
+            (w2_first_hbm, state2.at[1]),
+            (w2_second_hbm, state2.at[2]),
+            (w2_average_hbm, state2.at[3]),
+        )
+    ]
+    for load in rest:
+        load.start()
     loads[2].wait()
     loads[3].wait()
 
@@ -307,7 +321,16 @@
     shift_row = small_ref[9:10, :]
     scale = small_ref[14:15, :]
 
-    def forward_tile(b):
+    first_row = jnp.where(lax.broadcasted_iota(jnp.int32, (8, TILE), 0) == 0, 1.0, 0.0).astype(BF16)
+
+    def turn_tile(b):
+        row = pl.multiple_of(b * TILE, TILE)
+        nmt[:, pl.ds(row, TILE)] = nm[pl.ds(row, TILE), :].T
+        gbt[:, pl.ds(row, TILE)] = gb[pl.ds(row, TILE), :].T
+
+    def forward_tile(b, turned=None):
+        if turned is not None:
+            turn_tile(turned)
         row = pl.multiple_of(b * TILE, TILE)
         starts_here = flags[pl.ds(b, 1), :]
         ends_here = flags[pl.ds(b + 1, 1), :]
@@ -338,31 +361,27 @@
             nm[rows, :] = (unit * gain + shift_row).astype(BF16)
             low = (scale * ct[rows, :].astype(F32)).astype(BF16)
             gb[rows, :] = low
-            accs[10] += fold(low.astype(F32))
-        nmt[:, pl.ds(row, TILE)] = nm[pl.ds(row, TILE), :].T
-        gbt[:, pl.ds(row, TILE)] = gb[pl.ds(row, TILE), :].T
+        accs[10] += jnp.dot(first_row, gb[pl.ds(row, TILE), :], preferred_element_type=F32)
 
     def forward_tiles(low, high):
         @pl.loop(low, high)
         def _(b):
-            forward_tile(b)
+            forward_tile(b, b - 1)
 
     nb = p.nb
-    cut = [1 + (nb - 2) * i // 4 for i in range(5)]
+    cut = [2, nb * 3 // 8, nb * 5 // 8, nb * 7 // 8, nb]
+    forward_tile(1)
     forward_tiles(cut[0], cut[1])
     gather_one(0)
     forward_tiles(cut[1], cut[2])
+    gather_one(1)
+    forward_tiles(cut[2], cut[3])
     gather_two(0)
-    forward_tiles(cut[2], cut[3])
-    gather_one(1)
+    arrived(frx.at[pl.ds(HALO + t_len, HALO)], halo_sem.at[1])
     forward_tiles(cut[3], cut[4])
     arrived(frx.at[pl.ds(0, HALO)], halo_sem.at[0])
-    arrived(frx.at[pl.ds(HALO + t_len, HALO)], halo_sem.at[1])
-
-    @pl.loop(0, 2)
-    def _(i):
-        forward_tile(i * (nb - 1))
-
+    forward_tile(0, nb - 1)
+    turn_tile(0)
     near_wait(0)
 
     def parts_of(j):
@@ -374,15 +393,15 @@
         jo, size, _, _ = parts_of(j)
         out = []
         for slot, q in ((0, near), (1, both)):
-            out.append(remote(s1w1.at[:, q, :, pl.ds(jo, size)], r1w1.at[slot, :, :, pl.ds(jo, size)], send_sem.at[14 + j], rs_sem.at[j, 0], rows=near))
-            out.append(remote(s1w2.at[q, pl.ds(jo, size), :], r1w2.at[slot, pl.ds(jo, size), :], send_sem.at[14 + j], rs_sem.at[j, 0], rows=near))
+            out.append(remote(s1w1.at[:, q, :, pl.ds(jo, size)], r1w1.at[slot, :, :, pl.ds(jo, size)], send_sem.at[3, j], rs_sem.at[j, 0], rows=near))
+            out.append(remote(s1w2.at[q, pl.ds(jo, size), :], r1w2.at[slot, pl.ds(jo, size), :], send_sem.at[3, j], rs_sem.at[j, 0], rows=near))
         return out
 
     def cross_sends(j):
         jo, size, _, _ = parts_of(j)
         return [
-            remote(s2w1.at[:, :, pl.ds(jo, size)], r2w1.at[:, :, pl.ds(jo, size)], send_sem.at[18 + j], rs_sem.at[j, 1], rows=far),
-            remote(s2w2.at[pl.ds(jo, size), :], r2w2.at[pl.ds(jo, size), :], send_sem.at[18 + j], rs_sem.at[j, 1], rows=far),
+            remote(r1w1.at[1, :, :, pl.ds(jo, size)], r2w1.at[:, :, pl.ds(jo, size)], send_sem.at[4, j], rs_sem.at[j, 1], rows=far),
+            remote(r1w2.at[1, pl.ds(jo, size), :], r2w2.at[pl.ds(jo, size), :], send_sem.at[4, j], rs_sem.at[j, 1], rows=far),
         ]
 
     def holder_sends(j):
@@ -390,8 +409,8 @@
         out = []
         for step in range(1, nt):
             peer = (me_t + step) % nt
-            out.append(remote(s3w1.at[peer, :, pl.ds(jo, size)], r3w1.at[me_t, :, pl.ds(jo, size)], send_sem.at[22 + j], rs_sem.at[j, 2], tm=peer))
-            out.append(remote(s3w2.at[pl.ds(pl.multiple_of(jo + run * peer, run), run), :], r3w2.at[me_t, pl.ds(start_row, run), :], send_sem.at[22 + j], rs_sem.at[j, 2], tm=peer))
+            out.append(remote(r1w1.at[0, peer, :, pl.ds(jo, size)], r3w1.at[me_t, :, pl.ds(jo, size)], send_sem.at[5, j], rs_sem.at[j, 2], tm=peer))
+            out.append(remote(r1w2.at[0, pl.ds(pl.multiple_of(jo + run * peer, run), run), :], r3w2.at[me_t, pl.ds(start_row, run), :], send_sem.at[5, j], rs_sem.at[j, 2], tm=peer))
         return out
 
     def final_sends(j):
@@ -401,8 +420,8 @@
             peer = (me_r + step) % nr
             one = finw1.at[me_r, :, pl.ds(jo, size)]
             two = finw2.at[me_r, pl.ds(start_row, run), :]
-            out.append(remote(one, one, send_sem.at[26 + j], rs_sem.at[j, 3], rows=peer))
-            out.append(remote(two, two, send_sem.at[26 + j], rs_sem.at[j, 3], rows=peer))
+            out.append(remote(one, one, send_sem.at[6, j], rs_sem.at[j, 3], rows=peer))
+            out.append(remote(two, two, send_sem.at[6, j], rs_sem.at[j, 3], rows=peer))
         return out
 
     def sum_zero(j):
@@ -419,9 +438,9 @@
         cols = pl.ds(jo, size)
         arrived(s1w1.at[:, :, :, cols], rs_sem.at[j, 0])
         one = s1w1[:, far, :, cols].astype(F32) + r1w1[1, :, :, cols].astype(F32)
-        s2w1[:, :, cols] = one.astype(BF16)
+        r1w1[1, :, :, cols] = one.astype(BF16)
         two = s1w2[far, cols, :].astype(F32) + r1w2[1, cols, :].astype(F32)
-        s2w2[cols, :] = two.astype(BF16)
+        r1w2[1, cols, :] = two.astype(BF16)
         start(cross_sends(j))
 
     def sum_two(j):
@@ -429,11 +448,11 @@
         cols = pl.ds(jo, size)
         arrived(s1w1.at[:, pl.ds(0, 2), :, cols], rs_sem.at[j, 1])
         one = s1w1[:, me_r, :, cols].astype(F32) + r1w1[0, :, :, cols].astype(F32) + r2w1[:, :, cols].astype(F32)
-        s3w1[:, :, cols] = one.astype(BF16)
+        r1w1[0, :, :, cols] = one.astype(BF16)
         two = s1w2[me_r, cols, :].astype(F32) + r1w2[0, cols, :].astype(F32) + r2w2[cols, :].astype(F32)
-        s3w2[cols, :] = two.astype(BF16)
-        r3w1[me_t, :, cols] = s3w1[me_t, :, cols]
-        r3w2[me_t, pl.ds(start_row, run), :] = s3w2[pl.ds(pl.multiple_of(jo + run * me_t, run), run), :]
+        r1w2[0, cols, :] = two.astype(BF16)
+        r3w1[me_t, :, cols] = r1w1[0, me_t, :, cols]
+        r3w2[me_t, pl.ds(start_row, run), :] = r1w2[0, pl.ds(pl.multiple_of(jo + run * me_t, run), run), :]
         start(holder_sends(j))
 
     def sum_three(j):
@@ -485,37 +504,33 @@
             act = (hidden * prob).astype(BF16)
             grad_hidden = (grad_act * (prob + hidden * bell)).astype(BF16)
             accb[:, cols] += fold(grad_hidden.astype(F32))
-            rows_add(br, i, jnp.dot(act, w2, preferred_element_type=F32), j == 0)
+            branch = jnp.dot(act, w2, preferred_element_type=F32)
+            br[rows, :] = branch if j == 0 else br[rows, :] + branch
             back = lax.dot_general(
                 grad_hidden, w1, (((1,), (1,)), ((), ())), preferred_element_type=F32
             )
-            gn[rows, :] = back if j == 0 else gn[rows, :] + back
+            rows_add(gn, i, back, j == 0)
             acc1[:, 0:size] += jnp.dot(nmt[:, rows], grad_hidden, preferred_element_type=F32)
             acc2[:, 0:size] += jnp.dot(gbt[:, rows], act, preferred_element_type=F32)
 
-    main_block(0, [(1, lambda: gather_two(1)), (2, lambda: gather_one(2))])
+    def then(*calls):
+        return [(at, functools.partial(task, j)) for at, task, j in calls]
+
+    main_block(0, then((1, gather_two, 1), (2, gather_one, 2)))
     sum_zero(0)
     near_wait(1)
-    main_block(
-        1, [(0, lambda: gather_two(2)), (1, lambda: sum_one(0)), (1, lambda: gather_one(3)), (2, lambda: sum_two(0)), (2, lambda: gather_two(3))]
-    )
+    main_block(1, then((1, sum_one, 0), (2, gather_two, 2), (2, gather_one, 3)))
     sum_zero(1)
     near_wait(2)
-    main_block(2, [(0, lambda: sum_three(0)), (1, lambda: sum_one(1))])
+    main_block(2, then((1, sum_two, 0), (1, sum_one, 1), (1, gather_one, 4), (2, gather_two, 3)))
     sum_zero(2)
     sum_two(1)
     near_wait(3)
-    main_block(3, [(1, lambda: sum_one(2)), (2, lambda: sum_three(1))])
+    main_block(3, then((1, sum_one, 2), (1, gather_two, 4), (2, sum_three, 0)))
     sum_zero(3)
-    sum_two(2)
-
-    def output_copy(b):
-        rows = pl.ds(pl.multiple_of(b * TILE, TILE), TILE)
-        return pltpu.make_async_copy(nm.at[rows], output_hbm.at[0, rows], out_sem.at[0])
-
-    def ingrad_copy(b):
-        rows = pl.ds(pl.multiple_of(b * TILE, TILE), TILE)
-        return pltpu.make_async_copy(gb.at[rows], ingrad_hbm.at[0, rows], out_sem.at[1])
+    near_wait(4)
+    main_block(4, then((0, sum_three, 1), (1, sum_one, 3), (2, sum_two, 2)))
+    sum_zero(4)
 
     bias_two = small_ref[13:14, :]
 
@@ -525,30 +540,28 @@
         for q in range(TILE // step):
             rows = pl.ds(row + q * step, step)
             place = slice(GAP + q * step, GAP + q * step + step)
-            branch = jnp.concatenate([br[b, c, place, :] for c in range(p.nc)], axis=1) + bias_two
-            source = frx[pl.ds(row + HALO + q * step, step), :].astype(F32)
-            nm[rows, :] = (source + scale * branch).astype(BF16)
-            accs[11] += fold(ct[rows, :].astype(F32) * branch)
-            grad = gn[rows, :]
+            accs[11] += fold(ct[rows, :].astype(F32) * (br[rows, :] + bias_two))
+            grad = jnp.concatenate([gn[b, c, place, :] for c in range(p.nc)], axis=1)
             unit = xhat[rows, :].astype(F32)
-            accs[8] += fold(grad * unit)
+            both_of = grad * unit
+            accs[8] += fold(both_of)
             accs[9] += fold(grad)
             u = grad * gain
             mean_u = jnp.sum(u, axis=1, keepdims=True) * (1.0 / p.d)
-            mean_x = jnp.sum(u * unit, axis=1, keepdims=True) * (1.0 / p.d)
+            mean_x = jnp.sum(both_of * gain, axis=1, keepdims=True) * (1.0 / p.d)
             inverse = rstd[rows, :]
             inverse = jnp.concatenate([inverse] * p.nc, axis=1)
-            low = ((u - mean_u - unit * mean_x) * inverse).astype(BF16).astype(F32)
-            accs[7] += fold(low)
+            rounded = ((u - mean_u - unit * mean_x) * inverse).astype(BF16)
+            accs[7] += jnp.dot(first_row[:, 0:step], rounded, preferred_element_type=F32)
+            low = rounded.astype(F32)
             for c in range(p.nc):
-                br[b, c, place, :] = low[:, 128 * c : 128 * c + 128]
+                gn[b, c, place, :] = low[:, 128 * c : 128 * c + 128]
         for c in range(p.nc):
             cols = slice(128 * c, 128 * c + 128)
-            low = br[b, c, GAP : GAP + TILE, :]
+            low = gn[b, c, GAP : GAP + TILE, :]
             for k in range(TAPS):
                 first = GAP - 3 + k
                 accs[k, :, cols] += fold(low * xf[b, c, first : first + TILE, :])
-        output_copy(b).start()
 
     def backward_tiles(low, high):
         @pl.loop(low, high)
@@ -558,8 +571,8 @@
     def edge_sends():
         after, before = (me_t + 1) % nt, (me_t + nt - 1) % nt
         return [
-            remote(br.at[nb - 1, :, pl.ds(TILE, GAP), :], hprev, send_sem.at[30], halo_sem.at[2], tm=after),
-            remote(br.at[0, :, pl.ds(GAP, GAP), :], hnext, send_sem.at[31], halo_sem.at[3], tm=before),
+            remote(gn.at[nb - 1, :, pl.ds(TILE, GAP), :], hprev, send_sem.at[7, 2], halo_sem.at[2], tm=after),
+            remote(gn.at[0, :, pl.ds(GAP, GAP), :], hnext, send_sem.at[7, 3], halo_sem.at[3], tm=before),
         ]
 
     @pl.loop(0, 2)
@@ -567,14 +580,14 @@
         backward_tile(i * (nb - 1))
 
     start(edge_sends())
-    sum_one(3)
-    cut = [1 + (nb - 2) * i // 4 for i in range(5)]
+    sum_two(3)
+    cut = [1, 1 + (nb - 2) // 4, 1 + (nb - 2) * 3 // 4, nb - 1]
     backward_tiles(cut[0], cut[1])
+    sum_one(4)
+    backward_tiles(cut[1], cut[2])
     sum_three(2)
-    backward_tiles(cut[1], cut[2])
-    sum_two(3)
-    backward_tiles(cut[2], cut[4])
-    sum_three(3)
+    backward_tiles(cut[2], cut[3])
+    sum_two(4)
 
     hidden_tiles = lane_permuted(lambda i: accb[:, 128 * i : 128 * i + 128], p.regrouped, p.ff // 128)
     for c in range(p.nc):
@@ -593,21 +606,21 @@
         out = []
         for step in range(1, nr):
             peer = (me_r + step) % nr
-            out.append(remote(sma.at[peer], smr.at[me_r], send_sem.at[32], sm_sem.at[0], rows=peer))
+            out.append(remote(sma.at[peer], smr.at[me_r], send_sem.at[7, 4], sm_sem.at[0], rows=peer))
         return out
 
     def small_two_sends():
         out = []
         for step in range(1, nt):
             peer = (me_t + step) % nt
-            out.append(remote(smq.at[nt], smq.at[me_t], send_sem.at[33], sm_sem.at[1], tm=peer))
+            out.append(remote(smq.at[nt], smq.at[me_t], send_sem.at[8, 0], sm_sem.at[1], tm=peer))
         return out
 
     def small_three_sends():
         out = []
         for step in range(1, nr):
             peer = (me_r + step) % nr
-            out.append(remote(smf.at[me_r], smf.at[me_r], send_sem.at[34], sm_sem.at[2], rows=peer))
+            out.append(remote(smf.at[me_r], smf.at[me_r], send_sem.at[8, 1], sm_sem.at[2], rows=peer))
         return out
 
     smr[me_r] = sma[me_r]
@@ -633,43 +646,49 @@
     def exchange_edges(b):
         same = flags[pl.ds(b, 1), :] < 0.5
         for c in range(p.nc):
-            br[b, c, 0:GAP, :] = jnp.where(same, br[b - 1, c, TILE : TILE + GAP, :], 0.0)
-            br[b - 1, c, GAP + TILE :, :] = jnp.where(same, br[b, c, GAP : GAP + GAP, :], 0.0)
-
-    def input_tile(b):
+            gn[b, c, 0:GAP, :] = jnp.where(same, gn[b - 1, c, TILE : TILE + GAP, :], 0.0)
+            gn[b - 1, c, GAP + TILE :, :] = jnp.where(same, gn[b, c, GAP : GAP + GAP, :], 0.0)
+
+    def last_tile(b):
         row = pl.multiple_of(b * TILE, TILE)
+        rows = pl.ds(row, TILE)
         for c in range(p.nc):
             cols = slice(128 * c, 128 * c + 128)
-            total = ct[pl.ds(row, TILE), cols].astype(F32)
+            source = frx[pl.ds(row + HALO, TILE), cols].astype(F32)
+            branch = br[rows, cols] + bias_two[:, cols]
+            nm[rows, cols] = (source + scale[:, cols] * branch).astype(BF16)
+            total = ct[rows, cols].astype(F32)
             for k in range(TAPS):
                 first = GAP + 3 - k
-                total = total + small_ref[k : k + 1, cols] * br[b, c, first : first + TILE, :]
-            gb[pl.ds(row, TILE), cols] = total.astype(BF16)
-        ingrad_copy(b).start()
+                total = total + small_ref[k : k + 1, cols] * gn[b, c, first : first + TILE, :]
+            gb[rows, cols] = total.astype(BF16)
 
     exchange_edges(1)
 
-    def input_tiles(low, high):
+    def last_tiles(low, high):
         @pl.loop(low, high)
         def _(b):
             exchange_edges(b + 1)
-            input_tile(b)
-
-    cut = [1 + (nb - 2) * i // 4 for i in range(5)]
-    input_tiles(cut[0], cut[1])
+            last_tile(b)
+
+    cut = [1, 1 + (nb - 2) * 4 // 10, 1 + (nb - 2) * 7 // 10, nb - 1]
+    last_tiles(cut[0], cut[1])
     small_two()
-    input_tiles(cut[1], cut[3])
-    small_three()
-    input_tiles(cut[3], cut[4])
+    last_tiles(cut[1], cut[2])
+    sum_three(3)
+    last_tiles(cut[2], cut[3])
     arrived(hprev, halo_sem.at[2])
     arrived(hnext, halo_sem.at[3])
     for c in range(p.nc):
-        br[0, c, 0:GAP, :] = jnp.where(flags[0:1, :] < 0.5, hprev[c], 0.0)
-        br[nb - 1, c, GAP + TILE :, :] = jnp.where(flags[nb : nb + 1, :] < 0.5, hnext[c], 0.0)
+        gn[0, c, 0:GAP, :] = jnp.where(flags[0:1, :] < 0.5, hprev[c], 0.0)
+        gn[nb - 1, c, GAP + TILE :, :] = jnp.where(flags[nb : nb + 1, :] < 0.5, hnext[c], 0.0)
 
     @pl.loop(0, 2)
     def _(i):
-        input_tile(i * (nb - 1))
+        last_tile(i * (nb - 1))
+
+    small_three()
+    sum_three(4)
 
     for j in range(len(p.blocks)):
         sum_wait(j)
@@ -688,12 +707,80 @@
         sent += pair_sends(j) + cross_sends(j) + holder_sends(j) + final_sends(j)
     for copy in sent:
         copy.wait_send()
-    whole = pl.ds(0, t_len)
-    pltpu.make_async_copy(nm.at[whole], output_hbm.at[0, whole], out_sem.at[0]).wait()
-    pltpu.make_async_copy(gb.at[whole], ingrad_hbm.at[0, whole], out_sem.at[1]).wait()
-
-
-def call(plan, frames, cotangent, lengths, w1_master, w2_master, small_master):
+    for load in rest:
+        load.wait()
+
+
+def finish_kernel(
+    nm, gb, grad1, grad2, grad_small, state1, state2,
+    small_master, small_first, small_second, small_average,
+    output, ingrad, *rest,
+):
+    outs1, outs2, outs_small = rest[0:5], rest[5:10], rest[10:15]
+    new1, low1, new2, low2, sem = rest[15:]
+    copies = [
+        pltpu.make_async_copy(nm, output.at[0], sem.at[0]),
+        pltpu.make_async_copy(gb, ingrad.at[0], sem.at[1]),
+    ]
+    for copy in copies:
+        copy.start()
+    count = 2
+    for grad, state, new, low, outs, rate in (
+        (grad1, state1, new1, low1, outs1, rate_first),
+        (grad2, state2, new2, low2, outs2, rate_second),
+    ):
+        step = 32
+        for q in range(grad.shape[0] // step):
+            rows = slice(q * step, q * step + step)
+            got = adamw_step(
+                state[0, rows], state[1, rows], state[2, rows], state[3, rows], grad[rows], rate
+            )
+            for k in range(4):
+                new[k, rows] = got[k]
+            low[rows] = got[4]
+        for k in range(5):
+            source = low if k == 4 else new.at[k]
+            copy = pltpu.make_async_copy(source, outs[k], sem.at[count])
+            copy.start()
+            copies.append(copy)
+            count += 1
+    got = adamw_step(
+        small_master[...], small_first[...], small_second[...], small_average[...], grad_small[0:15], rate_small
+    )
+    for k in range(5):
+        outs_small[k][...] = got[k]
+    for copy in copies:
+        copy.wait()
+
+
+def finish(kept, smalls, t):
+    vmem = pl.BlockSpec(memory_space=pltpu.VMEM)
+    anyplace = pl.BlockSpec(memory_space=pl.ANY)
+    kept = [pltpu.with_memory_space_constraint(value, pltpu.VMEM) for value in kept]
+    nm, _, grad1, grad2 = kept[:4]
+    whole = jax.ShapeDtypeStruct((1, t, nm.shape[1]), BF16)
+
+    def five(shape):
+        return [jax.ShapeDtypeStruct(shape, F32)] * 4 + [jax.ShapeDtypeStruct(shape, BF16)]
+
+    v = pltpu.VMEM
+    return pl.pallas_call(
+        finish_kernel,
+        out_shape=(whole, whole, *five(grad1.shape), *five(grad2.shape), *five(smalls[0].shape)),
+        in_specs=[vmem] * 11,
+        out_specs=(anyplace,) * 12 + (vmem,) * 5,
+        scratch_shapes=[
+            v((4, *grad1.shape), F32),
+            v(grad1.shape, BF16),
+            v((4, *grad2.shape), F32),
+            v(grad2.shape, BF16),
+            pltpu.SemaphoreType.DMA((12,)),
+        ],
+        compiler_params=pltpu.CompilerParams(vmem_limit_bytes=8_000_000),
+    )(*kept, *smalls)
+
+
+def call(plan, frames, cotangent, lengths, one, two, small_master):
     p = plan
     t, d, ff, nt, nr, nb, nc = p.t, p.d, p.ff, p.nt, p.nr, p.nb, p.nc
     vmem = pl.BlockSpec(memory_space=pltpu.VMEM)
@@ -703,19 +790,15 @@
     scratch = [
         v((t + 2 * HALO, d), BF16),
         v((t, d), BF16),
-        v((t, d), BF16),
         v((d, t), BF16),
-        v((t, d), BF16),
         v((d, t), BF16),
+        v((t, d), F32),
         v((nb, nc, TILE + 2 * GAP, 128), F32),
-        v((t, d), F32),
         v((nb, nc, TILE + 2 * GAP, 128), F32),
         v((t, d), BF16),
         v((t, 128), F32),
         v((nt, nr, p.part, ff), BF16),
         v((nr, ff, p.lanes), BF16),
-        v((p.part, ff), F32),
-        v((p.share, p.lanes), F32),
         v((d, p.widest), F32),
         v((d, p.widest), F32),
         v((8, n_lens), F32),
@@ -731,10 +814,6 @@
         v((nt, p.part, ff), BF16),
         v((ff, p.lanes), BF16),
         v((nt, p.part, ff), BF16),
-        v((ff, p.lanes), BF16),
-        v((nt, p.part, ff), BF16),
-        v((ff, p.lanes), BF16),
-        v((nt, p.part, ff), BF16),
         v((nt, p.share, p.lanes), BF16),
         v((nr, p.part, ff), F32),
         v((nr, p.share, p.lanes), F32),
@@ -744,30 +823,31 @@
         v((nr, 16, p.lanes), F32),
         v((nc, GAP, 128), F32),
         v((nc, GAP, 128), F32),
+        pltpu.SemaphoreType.DMA((5,)),
+        pltpu.SemaphoreType.DMA((9, len(p.blocks))),
         pltpu.SemaphoreType.DMA((4,)),
-        pltpu.SemaphoreType.DMA((2,)),
-        pltpu.SemaphoreType.DMA((35,)),
-        pltpu.SemaphoreType.DMA((4,)),
-        pltpu.SemaphoreType.DMA((4, 3)),
-        pltpu.SemaphoreType.DMA((4, 4)),
+        pltpu.SemaphoreType.DMA((len(p.blocks), 3)),
+        pltpu.SemaphoreType.DMA((len(p.blocks), 4)),
         pltpu.SemaphoreType.DMA((3,)),
     ]
     return pl.pallas_call(
         functools.partial(kernel, plan),
         out_shape=(
-            jax.ShapeDtypeStruct((1, t, d), BF16),
-            jax.ShapeDtypeStruct((1, t, d), BF16),
-            jax.ShapeDtypeStruct((p.rows1, ff), F32),
-            jax.ShapeDtypeStruct((p.share, d), F32),
-            jax.ShapeDtypeStruct((16, d), F32),
+            v((t, d), BF16),
+            v((t, d), BF16),
+            v((p.rows1, ff), F32),
+            v((p.share, d), F32),
+            v((16, d), F32),
+            v((4, p.rows1, ff), F32),
+            v((4, p.share, d), F32),
         ),
-        in_specs=[anyplace, anyplace, vmem, anyplace, anyplace, vmem],
-        out_specs=(anyplace, anyplace, vmem, vmem, vmem),
+        in_specs=[anyplace, anyplace, vmem] + [anyplace] * 8 + [vmem],
+        out_specs=(vmem,) * 7,
         scratch_shapes=scratch,
         compiler_params=pltpu.CompilerParams(
-            collective_id=0, has_side_effects=True, vmem_limit_bytes=67_000_000
+            collective_id=0, has_side_effects=True, vmem_limit_bytes=56_500_000
         ),
-    )(frames, cotangent, lengths, w1_master, w2_master, small_master)
+    )(frames, cotangent, lengths, *one, *two, small_master)
 
 
 def padded_2(array, sides, width):
@@ -960,15 +1040,16 @@
 ):
     nt, nr = lax.axis_size("tm"), lax.axis_size("rows")
     plan = Plan(nt, nr, frames.shape[1], frames.shape[2], w1_master.shape[1])
-    output, input_grad, grad_one, grad_two, small_total = call(
-        plan, frames, cotangent, lengths, w1_master, w2_master, small_master
-    )
-    one_out = adamw_step(w1_master, w1_first, w1_second, w1_average, grad_one, rate_first)
-    two_out = adamw_step(w2_master, w2_first, w2_second, w2_average, grad_two, rate_second)
-    small_out = adamw_step(
-        small_master, small_first, small_second, small_average, small_total[:15], rate_small
-    )
-    return (output, input_grad, *one_out, *two_out, *small_out)
+    kept = call(
+        plan,
+        frames,
+        cotangent,
+        lengths,
+        (w1_master, w1_first, w1_second, w1_average),
+        (w2_master, w2_first, w2_second, w2_average),
+        small_master,
+    )
+    return finish(kept, (small_master, small_first, small_second, small_average), plan.t)
 
 
 def solution(mesh):

time: 109 us -> 90.5 us (0.83)
  Pallas kernels: 96.4 us -> 89.4 us
  other arithmetic: 6.73 us -> 0 us
  local copies, waits for them, and re-layouts: 4.76 us -> 0.02 us
    pallas_call x1 -> x2, Pallas kernels: 96.4 us -> 89.4 us  [the longest x1 84.9 us: call(): pl.pallas_call(functools.partial(kernel, plan), out_shape=(v((t, d), BF16...]
    unnamed x34 -> x8, local copies, waits for them, and re-layouts: 4.76 us -> 0.02 us
    convert_element_type x3 -> x0, other arithmetic: 4.44 us -> none  [adamw_step(): master_new.astype(BF16)]
    add x3 -> x0, other arithmetic: 2.29 us -> none  [adamw_step(): average_new = average_keep * average_old + (1.0 - average_keep) * master_new]
where the time goes in v2:
time: 90.5 us; the launch traced here: 90.3 us
  Pallas kernels  89.4 us (99%)
    pallas_call x1, Pallas kernels, call(): pl.pallas_call(functools.partial(kernel, plan), out_shape=(v((t, d), BF16...  84.9 us
    pallas_call x1, Pallas kernels, finish(): pl.pallas_call(finish_kernel, out_shape=(whole, whole, *five(grad1.shape)...  4.53 us

profile of v2, /device:TPU:0, one launch (start us, length us, event | category | flops | bytes accessed | tf_op | source)
XLA Modules:
  0.0 90.3 jit_solution(6159122996245071151)
XLA Ops:
  0.7 0.0 copy-start
  0.7 0.0 copy-start.3
  0.7 0.0 copy-start.2
  0.7 0.0 copy-start.1
  0.7 84.9 %shard_map.278 = (bf16[3072,512]{1,0:T(8,128)(2,1)S(1)}, bf16[3072,512]{1,0:T(8,128)(2,1)S(1)}, f32[64,1536]{1,0:T(8,128)S(1)}, f32[192,512]{1,0:T(8,128)S(1)}, ...) custom-call(bf16[1,3072,512]{2,1,0:T(8,128)(2,1)} %frames_hbm.1, ...), custom_call_target="tpu_custom_call" | custom-call | tf_op jit(solution)/shard_map/pallas_call | solution.py:833
  85.6 0.0 copy-done
  85.6 0.0 copy-done.3
  85.6 0.0 copy-done.2
  85.6 0.0 copy-done.1
  85.6 4.5 %shard_map.279 = (bf16[1,3072,512]{2,1,0:T(8,128)(2,1)}, bf16[1,3072,512]{2,1,0:T(8,128)(2,1)}, f32[64,1536]{1,0:T(8,128)}, f32[64,1536]{1,0:T(8,128)}, f32[64,1...) custom-call(bf16[3072,512]{1,0:T(8,128)(2,1)S(1)} %get-tuple-element, ...), custom_call_target="tpu_custom_call" | custom-call | tf_op jit(solution)/shard_map/pallas_call | solution.py:767
Async XLA Ops:
  0.7 84.9 %copy-start = (f32[15,512]{1,0:T(8,128)S(1)}, f32[15,512]{1,0:T(8,128)}, u32[]{:S(2)}) copy-start(f32[15,512]{1,0:T(8,128)} %small_master.1) | copy-start | bytes 92164
  0.7 84.9 %copy-start.3 = (f32[15,512]{1,0:T(8,128)S(1)}, f32[15,512]{1,0:T(8,128)}, u32[]{:S(2)}) copy-start(f32[15,512]{1,0:T(8,128)} %small_average.1) | copy-start | bytes 92164
  0.7 84.9 %copy-start.2 = (f32[15,512]{1,0:T(8,128)S(1)}, f32[15,512]{1,0:T(8,128)}, u32[]{:S(2)}) copy-start(f32[15,512]{1,0:T(8,128)} %small_second.1) | copy-start | bytes 92164
  0.7 84.9 %copy-start.1 = (f32[15,512]{1,0:T(8,128)S(1)}, f32[15,512]{1,0:T(8,128)}, u32[]{:S(2)}) copy-start(f32[15,512]{1,0:T(8,128)} %small_first.1) | copy-start | bytes 92164

commit v3 on v2

--- a/solution.py
+++ b/solution.py
@@ -22,7 +22,7 @@
 TAPS = 7
 TILE = 128
 GAP = 8
-GRAIN = 32
+GRAIN = 16
 HALO = 16
 F32 = jnp.float32
 BF16 = jnp.bfloat16
@@ -52,20 +52,23 @@
         self.lanes = width // nr
         self.nb = frame_count // TILE
         self.nc = width // 128
-        self.runs = [32, 32, 64, 32, 32]
-        self.starts = [0, 32, 64, 128, 160]
-        self.blocks = []
-        offset = 0
-        for run in self.runs:
-            self.blocks.append((offset, run * nt))
+        self.chunks = []
+        offset = begin = 0
+        for run in (16, 16, 32, 32, 32, 32, 32):
+            self.chunks.append((offset, run * nt, run, begin))
             offset += run * nt
+            begin += run
+        self.members = [(0, 1), (2,), (3, 4), (5, 6)]
+        self.blocks = [
+            (self.chunks[own[0]][0], sum(self.chunks[j][1] for j in own)) for own in self.members
+        ]
         self.widest = max(size for _, size in self.blocks)
         self.m = 1024
         self.natural = []
-        for run, start in zip(self.runs, self.starts):
+        for _, _, run, begin in self.chunks:
             for k in range(nt):
                 for o in range(0, run, GRAIN):
-                    self.natural.append((self.share * k + start + o) // GRAIN)
+                    self.natural.append((self.share * k + begin + o) // GRAIN)
         self.regrouped = [self.natural.index(g) for g in range(hidden // GRAIN)]
 
 
@@ -73,13 +76,16 @@
     per = 128 // GRAIN
     out = []
     for tile in range(count):
-        value = None
+        value, before = None, None
         for q in range(per):
             run = source[tile * per + q]
-            piece = tile_of(run // per)
-            shift = ((q - run % per) % per) * GRAIN
-            if shift:
-                piece = pltpu.roll(piece, shift, 1)
+            now = (run // per, (q - run % per) % per)
+            if now == before:
+                continue
+            before = now
+            piece = tile_of(now[0])
+            if now[1]:
+                piece = pltpu.roll(piece, now[1] * GRAIN, 1)
             if value is None:
                 value = piece
             else:
@@ -113,8 +119,8 @@
     small_ref,
     nm,
     gb,
-    g1_out,
-    g2_out,
+    finw1,
+    finw2,
     small_out,
     state1,
     state2,
@@ -145,8 +151,6 @@
     r2w2,
     r3w1,
     r3w2,
-    finw1,
-    finw2,
     sma,
     smr,
     smq,
@@ -228,8 +232,8 @@
     own1 = lane_permuted(lambda i: state1[0, own_rows, 128 * i : 128 * i + 128], p.natural, p.ff // 128)
     for i, tile in enumerate(own1):
         w1b[me_t, me_r, :, 128 * i : 128 * i + 128] = tile.astype(BF16)
-    for (jo, _), run, start in zip(p.blocks, p.runs, p.starts):
-        w2b[me_r, pl.ds(pl.multiple_of(jo + run * me_t, run), run), :] = state2[0, start : start + run, own_lanes].astype(BF16)
+    for jo, _, run, begin in p.chunks:
+        w2b[me_r, pl.ds(pl.multiple_of(jo + run * me_t, run), run), :] = state2[0, begin : begin + run, own_lanes].astype(BF16)
 
     pl.semaphore_wait(barrier, nt + nr - 2)
 
@@ -241,16 +245,15 @@
         ]
 
     def w1_part(j, q):
-        jo, size = p.blocks[j]
+        jo, size = p.chunks[j][:2]
         return w1b.at[:, q, :, pl.ds(jo, size)]
 
     def w2_part(j, q):
-        jo, size = p.blocks[j]
+        jo, size = p.chunks[j][:2]
         return w2b.at[q, pl.ds(jo, size), :]
 
     def spread_sends(j):
-        jo, size = p.blocks[j]
-        run = p.runs[j]
+        jo, size, run, _ = p.chunks[j]
         out = []
         for step in range(1, nt):
             peer = (me_t + step) % nt
@@ -261,7 +264,7 @@
         return out
 
     def spread_wait(j):
-        jo, size = p.blocks[j]
+        jo, size = p.chunks[j][:2]
         arrived(w1b.at[pl.ds(0, nt - 1), pl.ds(0, 2), :, pl.ds(jo, size)], ag_sem.at[j, 0])
 
     def far_sends(j):
@@ -271,7 +274,7 @@
         ]
 
     def far_wait(j):
-        jo, size = p.blocks[j]
+        jo, size = p.chunks[j][:2]
         arrived(w1b.at[:, pl.ds(0, 2), :, pl.ds(jo, size)], ag_sem.at[j, 1])
 
     def near_sends(j, q):
@@ -281,7 +284,7 @@
         ]
 
     def near_wait(j):
-        jo, size = p.blocks[j]
+        jo, size = p.chunks[j][:2]
         arrived(w1b.at[:, :, :, pl.ds(jo, size)], ag_sem.at[j, 2])
 
     def start(copies):
@@ -297,9 +300,12 @@
         far_wait(j)
         start(near_sends(j, far))
 
+    def spread(j):
+        start(spread_sends(j))
+
+    spread(0)
+    spread(1)
     start(halo_sends())
-    for j in range(len(p.blocks)):
-        start(spread_sends(j))
 
     rest = [
         pltpu.make_async_copy(source, target, in_sem.at[4])
@@ -369,25 +375,30 @@
             forward_tile(b, b - 1)
 
     nb = p.nb
-    cut = [2, nb * 3 // 8, nb * 5 // 8, nb * 7 // 8, nb]
     forward_tile(1)
-    forward_tiles(cut[0], cut[1])
+    forward_tiles(2, nb // 4 - 1)
+    spread(2)
+    forward_tiles(nb // 4 - 1, nb * 5 // 12)
     gather_one(0)
-    forward_tiles(cut[1], cut[2])
+    spread(3)
+    spread(4)
+    forward_tiles(nb * 5 // 12, nb * 7 // 12)
     gather_one(1)
-    forward_tiles(cut[2], cut[3])
+    forward_tiles(nb * 7 // 12, nb * 3 // 4)
     gather_two(0)
     arrived(frx.at[pl.ds(HALO + t_len, HALO)], halo_sem.at[1])
-    forward_tiles(cut[3], cut[4])
+    forward_tiles(nb * 3 // 4, nb)
+    gather_two(1)
+    gather_one(2)
     arrived(frx.at[pl.ds(0, HALO)], halo_sem.at[0])
     forward_tile(0, nb - 1)
     turn_tile(0)
     near_wait(0)
+    near_wait(1)
 
     def parts_of(j):
-        jo, size = p.blocks[j]
-        start_row, run = p.starts[j], p.runs[j]
-        return jo, size, start_row, run
+        jo, size, run, begin = p.chunks[j]
+        return jo, size, begin, run
 
     def pair_sends(j):
         jo, size, _, _ = parts_of(j)
@@ -424,14 +435,16 @@
             out.append(remote(two, two, send_sem.at[6, j], rs_sem.at[j, 3], rows=peer))
         return out
 
-    def sum_zero(j):
-        jo, size, _, _ = parts_of(j)
-        one = acc1[:, 0:size].astype(BF16).reshape(nt, nr, p.part, size)
-        s1w1[:, :, :, pl.ds(jo, size)] = one
-        two = acc2[:, 0:size].astype(BF16).T
-        for q in range(nr):
-            s1w2[q, pl.ds(jo, size), :] = two[:, p.lanes * q : p.lanes * q + p.lanes]
-        start(pair_sends(j))
+    def sum_zero(block):
+        first = p.blocks[block][0]
+        for j in p.members[block]:
+            jo, size, _, _ = parts_of(j)
+            cols = slice(jo - first, jo - first + size)
+            s1w1[:, :, :, pl.ds(jo, size)] = acc1[:, cols].astype(BF16).reshape(nt, nr, p.part, size)
+            two = acc2[:, cols].astype(BF16).T
+            for q in range(nr):
+                s1w2[q, pl.ds(jo, size), :] = two[:, p.lanes * q : p.lanes * q + p.lanes]
+            start(pair_sends(j))
 
     def sum_one(j):
         jo, size, _, _ = parts_of(j)
@@ -482,57 +495,90 @@
                 place = (i * per + s, c, slice(GAP, GAP + TILE), slice(None))
                 ref[place] = piece if first else ref[place] + piece
 
+    bias_two = small_ref[13:14, :]
+    last = len(p.blocks) - 1
+
+    def weights_of(j):
+        jo, size = p.blocks[j]
+        cols = pl.ds(jo, size)
+        w1 = w1b[:, :, :, cols].reshape(p.d, size)
+        return w1, jnp.concatenate([w2b[q, cols, :] for q in range(nr)], axis=1)
+
+    def back_dot(grad_hidden, w1):
+        return lax.dot_general(
+            grad_hidden, w1, (((1,), (1,)), ((), ())), preferred_element_type=F32
+        )
+
     def main_block(j, between):
         jo, size = p.blocks[j]
         cols = pl.ds(jo, size)
-        acc1[:, 0:size] = jnp.zeros((p.d, size), F32)
-        acc2[:, 0:size] = jnp.zeros((p.d, size), F32)
 
         @pl.loop(0, t_len // m)
         def _(i):
             for at, task in between:
                 pl.when(i == at)(task)
             rows = pl.ds(pl.multiple_of(i * m, m), m)
-            w1 = w1b[:, :, :, cols].reshape(p.d, size)
-            w2 = jnp.concatenate([w2b[q, cols, :] for q in range(nr)], axis=1)
+            w1, w2 = weights_of(j)
             hidden = jnp.dot(nm[rows, :], w1, preferred_element_type=F32) + b1p[0:1, cols]
-            grad_act = lax.dot_general(
-                gb[rows, :], w2, (((1,), (1,)), ((), ())), preferred_element_type=F32
-            )
+            grad_act = back_dot(gb[rows, :], w2)
             prob = 0.5 * (1.0 + lax.erf(hidden * RSQRT_HALF))
             bell = jnp.exp(hidden * hidden * np.float32(-0.5)) * RSQRT_2PI
             act = (hidden * prob).astype(BF16)
             grad_hidden = (grad_act * (prob + hidden * bell)).astype(BF16)
             accb[:, cols] += fold(grad_hidden.astype(F32))
-            branch = jnp.dot(act, w2, preferred_element_type=F32)
-            br[rows, :] = branch if j == 0 else br[rows, :] + branch
-            back = lax.dot_general(
-                grad_hidden, w1, (((1,), (1,)), ((), ())), preferred_element_type=F32
-            )
-            rows_add(gn, i, back, j == 0)
-            acc1[:, 0:size] += jnp.dot(nmt[:, rows], grad_hidden, preferred_element_type=F32)
-            acc2[:, 0:size] += jnp.dot(gbt[:, rows], act, preferred_element_type=F32)
+            if j == last:
+                nm[rows, 0:size] = act
+                gb[rows, 0:size] = grad_hidden
+            else:
+                branch = jnp.dot(act, w2, preferred_element_type=F32)
+                br[rows, :] = branch + bias_two if j == 0 else br[rows, :] + branch
+                rows_add(gn, i, back_dot(grad_hidden, w1), j == 0)
+            one = jnp.dot(nmt[:, rows], grad_hidden, preferred_element_type=F32)
+            two = jnp.dot(gbt[:, rows], act, preferred_element_type=F32)
+            acc1[:, 0:size] = one + jnp.where(i > 0, acc1[:, 0:size], 0.0)
+            acc2[:, 0:size] = two + jnp.where(i > 0, acc2[:, 0:size], 0.0)
 
     def then(*calls):
         return [(at, functools.partial(task, j)) for at, task, j in calls]
 
-    main_block(0, then((1, gather_two, 1), (2, gather_one, 2)))
+    main_block(0, then((1, gather_one, 3), (1, spread, 5), (1, spread, 6), (2, gather_two, 2), (2, gather_one, 4)))
     sum_zero(0)
-    near_wait(1)
-    main_block(1, then((1, sum_one, 0), (2, gather_two, 2), (2, gather_one, 3)))
+    near_wait(2)
+    main_block(
+        1,
+        then((1, sum_one, 0), (1, sum_one, 1), (1, gather_two, 3), (1, gather_one, 5), (2, gather_two, 4), (2, gather_one, 6)),
+    )
     sum_zero(1)
-    near_wait(2)
-    main_block(2, then((1, sum_two, 0), (1, sum_one, 1), (1, gather_one, 4), (2, gather_two, 3)))
+    near_wait(3)
+    near_wait(4)
+    main_block(
+        2,
+        then((1, sum_one, 2), (1, sum_two, 0), (1, sum_two, 1), (1, gather_two, 5), (2, gather_two, 6)),
+    )
     sum_zero(2)
-    sum_two(1)
-    near_wait(3)
-    main_block(3, then((1, sum_one, 2), (1, gather_two, 4), (2, sum_three, 0)))
+    sum_two(2)
+    sum_three(0)
+    sum_three(1)
+    near_wait(5)
+    near_wait(6)
+    main_block(3, then((1, sum_one, 3), (1, sum_one, 4)))
     sum_zero(3)
-    near_wait(4)
-    main_block(4, then((0, sum_three, 1), (1, sum_one, 3), (2, sum_two, 2)))
-    sum_zero(4)
-
-    bias_two = small_ref[13:14, :]
+    sum_two(3)
+    sum_three(2)
+
+    unit_rows = 2 * TILE
+
+    def backward_dots(u):
+        size = p.blocks[last][1]
+        rows = pl.ds(pl.multiple_of(u * unit_rows, unit_rows), unit_rows)
+        w1, w2 = weights_of(last)
+        branch = jnp.dot(nm[rows, 0:size], w2, preferred_element_type=F32)
+        br[rows, :] += branch
+        back = back_dot(gb[rows, 0:size], w1)
+        for s in range(2):
+            for c in range(p.nc):
+                piece = back[TILE * s : TILE * s + TILE, 128 * c : 128 * c + 128]
+                gn[2 * u + s, c, GAP : GAP + TILE, :] += piece
 
     def backward_tile(b):
         row = pl.multiple_of(b * TILE, TILE)
@@ -540,7 +586,7 @@
         for q in range(TILE // step):
             rows = pl.ds(row + q * step, step)
             place = slice(GAP + q * step, GAP + q * step + step)
-            accs[11] += fold(ct[rows, :].astype(F32) * (br[rows, :] + bias_two))
+            accs[11] += fold(ct[rows, :].astype(F32) * br[rows, :])
             grad = jnp.concatenate([gn[b, c, place, :] for c in range(p.nc)], axis=1)
             unit = xhat[rows, :].astype(F32)
             both_of = grad * unit
@@ -552,8 +598,8 @@
             inverse = rstd[rows, :]
             inverse = jnp.concatenate([inverse] * p.nc, axis=1)
             rounded = ((u - mean_u - unit * mean_x) * inverse).astype(BF16)
-            accs[7] += jnp.dot(first_row[:, 0:step], rounded, preferred_element_type=F32)
             low = rounded.astype(F32)
+            accs[7] += fold(low)
             for c in range(p.nc):
                 gn[b, c, place, :] = low[:, 128 * c : 128 * c + 128]
         for c in range(p.nc):
@@ -563,11 +609,6 @@
                 first = GAP - 3 + k
                 accs[k, :, cols] += fold(low * xf[b, c, first : first + TILE, :])
 
-    def backward_tiles(low, high):
-        @pl.loop(low, high)
-        def _(b):
-            backward_tile(b)
-
     def edge_sends():
         after, before = (me_t + 1) % nt, (me_t + nt - 1) % nt
         return [
@@ -575,19 +616,24 @@
             remote(gn.at[0, :, pl.ds(GAP, GAP), :], hnext, send_sem.at[7, 3], halo_sem.at[3], tm=before),
         ]
 
-    @pl.loop(0, 2)
-    def _(i):
-        backward_tile(i * (nb - 1))
+    backward_dots(0)
+    units = nb // 2
+
+    @pl.loop(0, units - 1)
+    def _(u):
+        for at, task in then(
+            (1, sum_one, 5), (1, sum_one, 6), (2, sum_two, 4), (6, sum_two, 5), (6, sum_three, 3), (8, sum_three, 4), (9, sum_two, 6)
+        ):
+            pl.when(u == at)(task)
+        backward_dots(u + 1)
+        backward_tile(2 * u)
+        backward_tile(2 * u + 1)
+
+    @pl.loop(nb - 2, nb)
+    def _(b):
+        backward_tile(b)
 
     start(edge_sends())
-    sum_two(3)
-    cut = [1, 1 + (nb - 2) // 4, 1 + (nb - 2) * 3 // 4, nb - 1]
-    backward_tiles(cut[0], cut[1])
-    sum_one(4)
-    backward_tiles(cut[1], cut[2])
-    sum_three(2)
-    backward_tiles(cut[2], cut[3])
-    sum_two(4)
 
     hidden_tiles = lane_permuted(lambda i: accb[:, 128 * i : 128 * i + 128], p.regrouped, p.ff // 128)
     for c in range(p.nc):
@@ -655,8 +701,7 @@
         for c in range(p.nc):
             cols = slice(128 * c, 128 * c + 128)
             source = frx[pl.ds(row + HALO, TILE), cols].astype(F32)
-            branch = br[rows, cols] + bias_two[:, cols]
-            nm[rows, cols] = (source + scale[:, cols] * branch).astype(BF16)
+            nm[rows, cols] = (source + scale[:, cols] * br[rows, cols]).astype(BF16)
             total = ct[rows, cols].astype(F32)
             for k in range(TAPS):
                 first = GAP + 3 - k
@@ -671,11 +716,12 @@
             exchange_edges(b + 1)
             last_tile(b)
 
-    cut = [1, 1 + (nb - 2) * 4 // 10, 1 + (nb - 2) * 7 // 10, nb - 1]
+    cut = [1, 1 + (nb - 2) // 2, 1 + (nb - 2) * 3 // 4, nb - 1]
     last_tiles(cut[0], cut[1])
     small_two()
+    sum_three(5)
     last_tiles(cut[1], cut[2])
-    sum_three(3)
+    sum_three(6)
     last_tiles(cut[2], cut[3])
     arrived(hprev, halo_sem.at[2])
     arrived(hnext, halo_sem.at[3])
@@ -688,21 +734,15 @@
         last_tile(i * (nb - 1))
 
     small_three()
-    sum_three(4)
-
-    for j in range(len(p.blocks)):
+
+    for j in range(len(p.chunks)):
         sum_wait(j)
-    for q in range(nr):
-        tiles = lane_permuted(lambda i, q=q: finw1[q, :, 128 * i : 128 * i + 128], p.regrouped, p.ff // 128)
-        for i, tile in enumerate(tiles):
-            g1_out[p.part * q : p.part * q + p.part, 128 * i : 128 * i + 128] = tile
-        g2_out[:, p.lanes * q : p.lanes * q + p.lanes] = finw2[q]
     arrived(smf.at[pl.ds(0, nr - 1)], sm_sem.at[2])
     for c in range(p.nc):
         small_out[:, 128 * c : 128 * c + 128] = smf[c]
 
     sent = halo_sends() + edge_sends() + small_one_sends() + small_two_sends() + small_three_sends()
-    for j in range(len(p.blocks)):
+    for j in range(len(p.chunks)):
         sent += spread_sends(j) + far_sends(j) + near_sends(j, me_r) + near_sends(j, far)
         sent += pair_sends(j) + cross_sends(j) + holder_sends(j) + final_sends(j)
     for copy in sent:
@@ -712,10 +752,12 @@
 
 
 def finish_kernel(
+    plan,
     nm, gb, grad1, grad2, grad_small, state1, state2,
     small_master, small_first, small_second, small_average,
     output, ingrad, *rest,
 ):
+    p = plan
     outs1, outs2, outs_small = rest[0:5], rest[5:10], rest[10:15]
     new1, low1, new2, low2, sem = rest[15:]
     copies = [
@@ -724,16 +766,26 @@
     ]
     for copy in copies:
         copy.start()
+
+    def first_grad(q):
+        tiles = lane_permuted(
+            lambda i: grad1[q, :, 128 * i : 128 * i + 128], p.regrouped, p.ff // 128
+        )
+        return jnp.concatenate(tiles, axis=1)
+
+    def second_grad(q):
+        rows = slice(q * p.part, q * p.part + p.part)
+        return jnp.concatenate([grad2[k, rows, :] for k in range(p.nr)], axis=1)
+
     count = 2
     for grad, state, new, low, outs, rate in (
-        (grad1, state1, new1, low1, outs1, rate_first),
-        (grad2, state2, new2, low2, outs2, rate_second),
+        (first_grad, state1, new1, low1, outs1, rate_first),
+        (second_grad, state2, new2, low2, outs2, rate_second),
     ):
-        step = 32
-        for q in range(grad.shape[0] // step):
-            rows = slice(q * step, q * step + step)
+        for q in range(low.shape[0] // p.part):
+            rows = slice(q * p.part, q * p.part + p.part)
             got = adamw_step(
-                state[0, rows], state[1, rows], state[2, rows], state[3, rows], grad[rows], rate
+                state[0, rows], state[1, rows], state[2, rows], state[3, rows], grad(q), rate
             )
             for k in range(4):
                 new[k, rows] = got[k]
@@ -753,27 +805,27 @@
         copy.wait()
 
 
-def finish(kept, smalls, t):
+def finish(plan, kept, smalls):
     vmem = pl.BlockSpec(memory_space=pltpu.VMEM)
     anyplace = pl.BlockSpec(memory_space=pl.ANY)
     kept = [pltpu.with_memory_space_constraint(value, pltpu.VMEM) for value in kept]
-    nm, _, grad1, grad2 = kept[:4]
-    whole = jax.ShapeDtypeStruct((1, t, nm.shape[1]), BF16)
+    shape1, shape2 = (plan.rows1, plan.ff), (plan.share, plan.d)
+    whole = jax.ShapeDtypeStruct((1, plan.t, plan.d), BF16)
 
     def five(shape):
         return [jax.ShapeDtypeStruct(shape, F32)] * 4 + [jax.ShapeDtypeStruct(shape, BF16)]
 
     v = pltpu.VMEM
     return pl.pallas_call(
-        finish_kernel,
-        out_shape=(whole, whole, *five(grad1.shape), *five(grad2.shape), *five(smalls[0].shape)),
+        functools.partial(finish_kernel, plan),
+        out_shape=(whole, whole, *five(shape1), *five(shape2), *five(smalls[0].shape)),
         in_specs=[vmem] * 11,
         out_specs=(anyplace,) * 12 + (vmem,) * 5,
         scratch_shapes=[
-            v((4, *grad1.shape), F32),
-            v(grad1.shape, BF16),
-            v((4, *grad2.shape), F32),
-            v(grad2.shape, BF16),
+            v((4, *shape1), F32),
+            v(shape1, BF16),
+            v((4, *shape2), F32),
+            v(shape2, BF16),
             pltpu.SemaphoreType.DMA((12,)),
         ],
         compiler_params=pltpu.CompilerParams(vmem_limit_bytes=8_000_000),
@@ -815,8 +867,6 @@
         v((ff, p.lanes), BF16),
         v((nt, p.part, ff), BF16),
         v((nt, p.share, p.lanes), BF16),
-        v((nr, p.part, ff), F32),
-        v((nr, p.share, p.lanes), F32),
         v((nr, 16, p.lanes), F32),
         v((nr, 16, p.lanes), F32),
         v((nt + 1, 16, p.lanes), F32),
@@ -824,10 +874,10 @@
         v((nc, GAP, 128), F32),
         v((nc, GAP, 128), F32),
         pltpu.SemaphoreType.DMA((5,)),
-        pltpu.SemaphoreType.DMA((9, len(p.blocks))),
+        pltpu.SemaphoreType.DMA((9, len(p.chunks))),
         pltpu.SemaphoreType.DMA((4,)),
-        pltpu.SemaphoreType.DMA((len(p.blocks), 3)),
-        pltpu.SemaphoreType.DMA((len(p.blocks), 4)),
+        pltpu.SemaphoreType.DMA((len(p.chunks), 3)),
+        pltpu.SemaphoreType.DMA((len(p.chunks), 4)),
         pltpu.SemaphoreType.DMA((3,)),
     ]
     return pl.pallas_call(
@@ -835,8 +885,8 @@
         out_shape=(
             v((t, d), BF16),
             v((t, d), BF16),
-            v((p.rows1, ff), F32),
-            v((p.share, d), F32),
+            v((nr, p.part, ff), F32),
+            v((nr, p.share, p.lanes), F32),
             v((16, d), F32),
             v((4, p.rows1, ff), F32),
             v((4, p.share, d), F32),
@@ -1049,7 +1099,7 @@
         (w2_master, w2_first, w2_second, w2_average),
         small_master,
     )
-    return finish(kept, (small_master, small_first, small_second, small_average), plan.t)
+    return finish(plan, kept, (small_master, small_first, small_second, small_average))
 
 
 def solution(mesh):

time: 90.5 us -> 82.6 us (0.913)
  Pallas kernels: 89.4 us -> 81.5 us
    pallas_call x1, Pallas kernels: 84.9 us -> 76.6 us  [call(): pl.pallas_call(functools.partial(kernel, plan), out_shape=(v((t, d), BF16...]
where the time goes in v3:
time: 82.6 us; the launch traced here: 82.4 us
  Pallas kernels  81.5 us (99%)
  between operations  0.89 us (1%)
    pallas_call x1, Pallas kernels, call(): pl.pallas_call(functools.partial(kernel, plan), out_shape=(v((t, d), BF16...  76.6 us
    pallas_call x1, Pallas kernels, finish(): pl.pallas_call(functools.partial(finish_kernel, plan), out_shape=(whole,...  4.89 us

profile of v3, /device:TPU:0, one launch (start us, length us, event | category | flops | bytes accessed | tf_op | source)
XLA Modules:
  0.0 82.4 jit_solution(1747434269301935559)
XLA Ops:
  0.7 0.0 copy-start
  0.7 0.0 copy-start.3
  0.7 0.0 copy-start.2
  0.7 0.0 copy-start.1
  0.7 76.6 %shard_map.278 = (bf16[3072,512]{1,0:T(8,128)(2,1)S(1)}, bf16[3072,512]{1,0:T(8,128)(2,1)S(1)}, f32[4,16,1536]{2,1,0:T(8,128)S(1)}, f32[4,192,128]{2,1,0:T(8,128...) custom-call(bf16[1,3072,512]{2,1,0:T(8,128)(2,1)} %frames_hbm.1, ...), custom_call_target="tpu_custom_call" | custom-call | tf_op jit(solution)/shard_map/pallas_call | solution.py:883
  77.3 0.0 copy-done
  77.4 0.0 copy-done.3
  77.4 0.0 copy-done.2
  77.4 0.0 copy-done.1
  77.4 4.9 %shard_map.279 = (bf16[1,3072,512]{2,1,0:T(8,128)(2,1)}, bf16[1,3072,512]{2,1,0:T(8,128)(2,1)}, f32[64,1536]{1,0:T(8,128)}, f32[64,1536]{1,0:T(8,128)}, f32[64,1...) custom-call(bf16[3072,512]{1,0:T(8,128)(2,1)S(1)} %get-tuple-element, ...), custom_call_target="tpu_custom_call" | custom-call | tf_op jit(solution)/shard_map/pallas_call | solution.py:819
Async XLA Ops:
  0.7 76.7 %copy-start = (f32[15,512]{1,0:T(8,128)S(1)}, f32[15,512]{1,0:T(8,128)}, u32[]{:S(2)}) copy-start(f32[15,512]{1,0:T(8,128)} %small_master.1) | copy-start | bytes 92164
  0.7 76.7 %copy-start.3 = (f32[15,512]{1,0:T(8,128)S(1)}, f32[15,512]{1,0:T(8,128)}, u32[]{:S(2)}) copy-start(f32[15,512]{1,0:T(8,128)} %small_average.1) | copy-start | bytes 92164
  0.7 76.7 %copy-start.2 = (f32[15,512]{1,0:T(8,128)S(1)}, f32[15,512]{1,0:T(8,128)}, u32[]{:S(2)}) copy-start(f32[15,512]{1,0:T(8,128)} %small_second.1) | copy-start | bytes 92164
  0.7 76.7 %copy-start.1 = (f32[15,512]{1,0:T(8,128)S(1)}, f32[15,512]{1,0:T(8,128)}, u32[]{:S(2)}) copy-start(f32[15,512]{1,0:T(8,128)} %small_first.1) | copy-start | bytes 92164

commit v4 on v3

--- a/solution.py
+++ b/solution.py
@@ -107,7 +107,7 @@
     plan,
     frames_hbm,
     cot_hbm,
-    lengths_ref,
+    lengths_hbm,
     w1_hbm,
     w1_first_hbm,
     w1_second_hbm,
@@ -116,7 +116,7 @@
     w2_first_hbm,
     w2_second_hbm,
     w2_average_hbm,
-    small_ref,
+    small_hbm,
     nm,
     gb,
     finw1,
@@ -137,6 +137,8 @@
     w2b,
     acc1,
     acc2,
+    lengths_ref,
+    small_ref,
     lens,
     flags,
     b1p,
@@ -187,9 +189,11 @@
         pltpu.make_async_copy(w2_hbm, state2.at[0], in_sem.at[1]),
         pltpu.make_async_copy(frames_hbm.at[0], frx.at[pl.ds(HALO, t_len)], in_sem.at[2]),
         pltpu.make_async_copy(cot_hbm.at[0], ct, in_sem.at[3]),
+        pltpu.make_async_copy(lengths_hbm, lengths_ref, in_sem.at[5]),
+        pltpu.make_async_copy(small_hbm, small_ref, in_sem.at[6]),
     ]
-    for load in loads:
-        load.start()
+    for k in (0, 1, 5, 4, 2, 3):
+        loads[k].start()
 
     barrier = pltpu.get_barrier_semaphore()
     for step in range(1, nt):
@@ -201,6 +205,8 @@
             barrier, inc=1, device_id={"tm": me_t, "rows": (me_r + step) % nr}, device_id_type=MESH
         )
 
+    loads[4].wait()
+    loads[5].wait()
     lens[...] = jnp.zeros_like(lens)
     n_len = lengths_ref.shape[1]
     lens[0:1, 0:n_len] = lengths_ref[...].astype(F32)
@@ -216,7 +222,8 @@
     edge = jnp.max(jnp.where(hit, 1.0, 0.0), axis=1, keepdims=True)
     flags[...] = jnp.broadcast_to(edge, flags.shape)
     accs[...] = jnp.zeros_like(accs)
-    accb[...] = jnp.zeros_like(accb)
+    ones_row = lax.broadcasted_iota(jnp.int32, (16, t_len), 0) == 0
+    nmt[p.d :, :] = jnp.where(ones_row, 1.0, 0.0).astype(BF16)
     bias_tiles = lane_permuted(
         lambda i: jnp.broadcast_to(small_ref[10 + i // p.nc : 11 + i // p.nc, 128 * (i % p.nc) : 128 * (i % p.nc) + 128], (8, 128)),
         p.natural,
@@ -263,9 +270,9 @@
             out.append(remote(two, two, send_sem.at[0, j], ag_sem.at[j, 0], tm=peer))
         return out
 
-    def spread_wait(j):
+    def spread_wait(j, sem=None):
         jo, size = p.chunks[j][:2]
-        arrived(w1b.at[pl.ds(0, nt - 1), pl.ds(0, 2), :, pl.ds(jo, size)], ag_sem.at[j, 0])
+        arrived(w1b.at[pl.ds(0, nt - 1), pl.ds(0, 2), :, pl.ds(jo, size)], ag_sem.at[j, 0] if sem is None else sem)
 
     def far_sends(j):
         return [
@@ -273,9 +280,9 @@
             remote(w2_part(j, me_r), w2_part(j, me_r), send_sem.at[1, j], ag_sem.at[j, 1], rows=far),
         ]
 
-    def far_wait(j):
+    def far_wait(j, sem=None):
         jo, size = p.chunks[j][:2]
-        arrived(w1b.at[:, pl.ds(0, 2), :, pl.ds(jo, size)], ag_sem.at[j, 1])
+        arrived(w1b.at[:, pl.ds(0, 2), :, pl.ds(jo, size)], ag_sem.at[j, 1] if sem is None else sem)
 
     def near_sends(j, q):
         return [
@@ -283,9 +290,9 @@
             remote(w2_part(j, q), w2_part(j, q), send_sem.at[2, j], ag_sem.at[j, 2], rows=near),
         ]
 
-    def near_wait(j):
+    def near_wait(j, sem=None):
         jo, size = p.chunks[j][:2]
-        arrived(w1b.at[:, :, :, pl.ds(jo, size)], ag_sem.at[j, 2])
+        arrived(w1b.at[:, :, :, pl.ds(jo, size)], ag_sem.at[j, 2] if sem is None else sem)
 
     def start(copies):
         for copy in copies:
@@ -331,7 +338,7 @@
 
     def turn_tile(b):
         row = pl.multiple_of(b * TILE, TILE)
-        nmt[:, pl.ds(row, TILE)] = nm[pl.ds(row, TILE), :].T
+        nmt[0 : p.d, pl.ds(row, TILE)] = nm[pl.ds(row, TILE), :].T
         gbt[:, pl.ds(row, TILE)] = gb[pl.ds(row, TILE), :].T
 
     def forward_tile(b, turned=None):
@@ -435,12 +442,25 @@
             out.append(remote(two, two, send_sem.at[6, j], rs_sem.at[j, 3], rows=peer))
         return out
 
+    def reduced(j, kind, sem=None):
+        jo, size, _, _ = parts_of(j)
+        view = s1w1.at[:, :, :, pl.ds(jo, size)]
+        if kind == 1:
+            view = s1w1.at[:, pl.ds(0, 2), :, pl.ds(jo, size)]
+        elif kind == 2:
+            view = s1w1.at[pl.ds(0, nt - 1), pl.ds(0, 2), :, pl.ds(jo, size)]
+        elif kind == 3:
+            view = s1w1.at[pl.ds(0, 3 * nt // 4), pl.ds(0, 2), :, pl.ds(jo, size)]
+        arrived(view, rs_sem.at[j, kind] if sem is None else sem)
+
     def sum_zero(block):
         first = p.blocks[block][0]
         for j in p.members[block]:
             jo, size, _, _ = parts_of(j)
             cols = slice(jo - first, jo - first + size)
-            s1w1[:, :, :, pl.ds(jo, size)] = acc1[:, cols].astype(BF16).reshape(nt, nr, p.part, size)
+            one = acc1[0 : p.d, cols].astype(BF16)
+            s1w1[:, :, :, pl.ds(jo, size)] = one.reshape(nt, nr, p.part, size)
+            accb[:, pl.ds(jo, size)] = acc1[p.d : p.d + 8, cols]
             two = acc2[:, cols].astype(BF16).T
             for q in range(nr):
                 s1w2[q, pl.ds(jo, size), :] = two[:, p.lanes * q : p.lanes * q + p.lanes]
@@ -449,7 +469,7 @@
     def sum_one(j):
         jo, size, _, _ = parts_of(j)
         cols = pl.ds(jo, size)
-        arrived(s1w1.at[:, :, :, cols], rs_sem.at[j, 0])
+        reduced(j, 0)
         one = s1w1[:, far, :, cols].astype(F32) + r1w1[1, :, :, cols].astype(F32)
         r1w1[1, :, :, cols] = one.astype(BF16)
         two = s1w2[far, cols, :].astype(F32) + r1w2[1, cols, :].astype(F32)
@@ -459,7 +479,7 @@
     def sum_two(j):
         jo, size, start_row, run = parts_of(j)
         cols = pl.ds(jo, size)
-        arrived(s1w1.at[:, pl.ds(0, 2), :, cols], rs_sem.at[j, 1])
+        reduced(j, 1)
         one = s1w1[:, me_r, :, cols].astype(F32) + r1w1[0, :, :, cols].astype(F32) + r2w1[:, :, cols].astype(F32)
         r1w1[0, :, :, cols] = one.astype(BF16)
         two = s1w2[me_r, cols, :].astype(F32) + r1w2[0, cols, :].astype(F32) + r2w2[cols, :].astype(F32)
@@ -471,7 +491,7 @@
     def sum_three(j):
         jo, size, start_row, run = parts_of(j)
         cols = pl.ds(jo, size)
-        arrived(s1w1.at[pl.ds(0, nt - 1), pl.ds(0, 2), :, cols], rs_sem.at[j, 2])
+        reduced(j, 2)
         one = r3w1[0, :, cols].astype(F32)
         two = r3w2[0, pl.ds(start_row, run), :].astype(F32)
         for k in range(1, nt):
@@ -482,8 +502,7 @@
         start(final_sends(j))
 
     def sum_wait(j):
-        jo, size, _, _ = parts_of(j)
-        arrived(s1w1.at[pl.ds(0, 3 * nt // 4), pl.ds(0, 2), :, pl.ds(jo, size)], rs_sem.at[j, 3])
+        reduced(j, 3)
 
     m = p.m
     per = m // TILE
@@ -525,7 +544,6 @@
             bell = jnp.exp(hidden * hidden * np.float32(-0.5)) * RSQRT_2PI
             act = (hidden * prob).astype(BF16)
             grad_hidden = (grad_act * (prob + hidden * bell)).astype(BF16)
-            accb[:, cols] += fold(grad_hidden.astype(F32))
             if j == last:
                 nm[rows, 0:size] = act
                 gb[rows, 0:size] = grad_hidden
@@ -737,15 +755,18 @@
 
     for j in range(len(p.chunks)):
         sum_wait(j)
+        spread_wait(j, send_sem.at[0, j])
+        far_wait(j, send_sem.at[1, j])
+        near_wait(j, send_sem.at[2, j])
+        for kind in range(4):
+            reduced(j, kind, send_sem.at[3 + kind, j])
+    for copy in halo_sends() + edge_sends():
+        copy.wait_send()
     arrived(smf.at[pl.ds(0, nr - 1)], sm_sem.at[2])
     for c in range(p.nc):
         small_out[:, 128 * c : 128 * c + 128] = smf[c]
 
-    sent = halo_sends() + edge_sends() + small_one_sends() + small_two_sends() + small_three_sends()
-    for j in range(len(p.chunks)):
-        sent += spread_sends(j) + far_sends(j) + near_sends(j, me_r) + near_sends(j, far)
-        sent += pair_sends(j) + cross_sends(j) + holder_sends(j) + final_sends(j)
-    for copy in sent:
+    for copy in small_one_sends() + small_two_sends() + small_three_sends():
         copy.wait_send()
     for load in rest:
         load.wait()
@@ -759,7 +780,7 @@
 ):
     p = plan
     outs1, outs2, outs_small = rest[0:5], rest[5:10], rest[10:15]
-    new1, low1, new2, low2, sem = rest[15:]
+    new1, low1, new2, low2, new_small, low_small, sem = rest[15:]
     copies = [
         pltpu.make_async_copy(nm, output.at[0], sem.at[0]),
         pltpu.make_async_copy(gb, ingrad.at[0], sem.at[1]),
@@ -778,6 +799,16 @@
         return jnp.concatenate([grad2[k, rows, :] for k in range(p.nr)], axis=1)
 
     count = 2
+    got = adamw_step(
+        small_master[...], small_first[...], small_second[...], small_average[...], grad_small[0:15], rate_small
+    )
+    for k in range(5):
+        source = low_small if k == 4 else new_small.at[k]
+        source[...] = got[k]
+        copy = pltpu.make_async_copy(source, outs_small[k], sem.at[count])
+        copy.start()
+        copies.append(copy)
+        count += 1
     for grad, state, new, low, outs, rate in (
         (first_grad, state1, new1, low1, outs1, rate_first),
         (second_grad, state2, new2, low2, outs2, rate_second),
@@ -796,11 +827,6 @@
             copy.start()
             copies.append(copy)
             count += 1
-    got = adamw_step(
-        small_master[...], small_first[...], small_second[...], small_average[...], grad_small[0:15], rate_small
-    )
-    for k in range(5):
-        outs_small[k][...] = got[k]
     for copy in copies:
         copy.wait()
 
@@ -820,13 +846,15 @@
         functools.partial(finish_kernel, plan),
         out_shape=(whole, whole, *five(shape1), *five(shape2), *five(smalls[0].shape)),
         in_specs=[vmem] * 11,
-        out_specs=(anyplace,) * 12 + (vmem,) * 5,
+        out_specs=(anyplace,) * 17,
         scratch_shapes=[
             v((4, *shape1), F32),
             v(shape1, BF16),
             v((4, *shape2), F32),
             v(shape2, BF16),
-            pltpu.SemaphoreType.DMA((12,)),
+            v((4, *smalls[0].shape), F32),
+            v(smalls[0].shape, BF16),
+            pltpu.SemaphoreType.DMA((17,)),
         ],
         compiler_params=pltpu.CompilerParams(vmem_limit_bytes=8_000_000),
     )(*kept, *smalls)
@@ -842,7 +870,7 @@
     scratch = [
         v((t + 2 * HALO, d), BF16),
         v((t, d), BF16),
-        v((d, t), BF16),
+        v((d + 16, t), BF16),
         v((d, t), BF16),
         v((t, d), F32),
         v((nb, nc, TILE + 2 * GAP, 128), F32),
@@ -851,8 +879,10 @@
         v((t, 128), F32),
         v((nt, nr, p.part, ff), BF16),
         v((nr, ff, p.lanes), BF16),
+        v((d + 16, p.widest), F32),
         v((d, p.widest), F32),
-        v((d, p.widest), F32),
+        v(lengths.shape, jnp.int32),
+        v(small_master.shape, F32),
         v((8, n_lens), F32),
         v((-(-(nb + 1) // 8) * 8, 128), F32),
         v((8, ff), F32),
@@ -873,7 +903,7 @@
         v((nr, 16, p.lanes), F32),
         v((nc, GAP, 128), F32),
         v((nc, GAP, 128), F32),
-        pltpu.SemaphoreType.DMA((5,)),
+        pltpu.SemaphoreType.DMA((7,)),
         pltpu.SemaphoreType.DMA((9, len(p.chunks))),
         pltpu.SemaphoreType.DMA((4,)),
         pltpu.SemaphoreType.DMA((len(p.chunks), 3)),
@@ -891,7 +921,7 @@
             v((4, p.rows1, ff), F32),
             v((4, p.share, d), F32),
         ),
-        in_specs=[anyplace, anyplace, vmem] + [anyplace] * 8 + [vmem],
+        in_specs=[anyplace] * 12,
         out_specs=(vmem,) * 7,
         scratch_shapes=scratch,
         compiler_params=pltpu.CompilerParams(

time: 82.6 us -> 80.7 us (0.977)
  Pallas kernels: 81.5 us -> 79.6 us
    pallas_call x1, Pallas kernels: 76.6 us -> 75.3 us  [call(): pl.pallas_call(functools.partial(kernel, plan), out_shape=(v((t, d), BF16...]
where the time goes in v4:
time: 80.7 us; the launch traced here: 80.5 us
  Pallas kernels  79.6 us (99%)
  between operations  0.89 us (1%)
    pallas_call x1, Pallas kernels, call(): pl.pallas_call(functools.partial(kernel, plan), out_shape=(v((t, d), BF16...  75.3 us
    pallas_call x1, Pallas kernels, finish(): pl.pallas_call(functools.partial(finish_kernel, plan), out_shape=(whole,...  4.37 us

profile of v4, /device:TPU:0, one launch (start us, length us, event | category | flops | bytes accessed | tf_op | source)
XLA Modules:
  0.0 80.5 jit_solution(2710430879885134989)
XLA Ops:
  0.7 0.0 copy-start
  0.7 0.0 copy-start.3
  0.7 0.0 copy-start.2
  0.7 0.0 copy-start.1
  0.7 75.3 %shard_map.278 = (bf16[3072,512]{1,0:T(8,128)(2,1)S(1)}, bf16[3072,512]{1,0:T(8,128)(2,1)S(1)}, f32[4,16,1536]{2,1,0:T(8,128)S(1)}, f32[4,192,128]{2,1,0:T(8,128...) custom-call(bf16[1,3072,512]{2,1,0:T(8,128)(2,1)} %frames_hbm.1, ...), custom_call_target="tpu_custom_call" | custom-call | tf_op jit(solution)/shard_map/pallas_call | solution.py:913
  76.0 0.0 copy-done
  76.0 0.0 copy-done.3
  76.0 0.0 copy-done.2
  76.0 0.0 copy-done.1
  76.0 4.4 %shard_map.279 = (bf16[1,3072,512]{2,1,0:T(8,128)(2,1)}, bf16[1,3072,512]{2,1,0:T(8,128)(2,1)}, f32[64,1536]{1,0:T(8,128)}, f32[64,1536]{1,0:T(8,128)}, f32[64,1...) custom-call(bf16[3072,512]{1,0:T(8,128)(2,1)S(1)} %get-tuple-element, ...), custom_call_target="tpu_custom_call" | custom-call | tf_op jit(solution)/shard_map/pallas_call | solution.py:845
Async XLA Ops:
  0.7 75.3 %copy-start = (f32[15,512]{1,0:T(8,128)S(1)}, f32[15,512]{1,0:T(8,128)}, u32[]{:S(2)}) copy-start(f32[15,512]{1,0:T(8,128)} %small_master.1) | copy-start | bytes 92164
  0.7 75.3 %copy-start.3 = (f32[15,512]{1,0:T(8,128)S(1)}, f32[15,512]{1,0:T(8,128)}, u32[]{:S(2)}) copy-start(f32[15,512]{1,0:T(8,128)} %small_average.1) | copy-start | bytes 92164
  0.7 75.3 %copy-start.2 = (f32[15,512]{1,0:T(8,128)S(1)}, f32[15,512]{1,0:T(8,128)}, u32[]{:S(2)}) copy-start(f32[15,512]{1,0:T(8,128)} %small_second.1) | copy-start | bytes 92164
  0.7 75.3 %copy-start.1 = (f32[15,512]{1,0:T(8,128)S(1)}, f32[15,512]{1,0:T(8,128)}, u32[]{:S(2)}) copy-start(f32[15,512]{1,0:T(8,128)} %small_first.1) | copy-start | bytes 92164

commit v5 on v4

--- a/solution.py
+++ b/solution.py
@@ -174,6 +174,11 @@
     far = (me_r + 2) % nr
     both = near + 2 - 4 * (near // 2)
 
+    upper = me_t // (nt // 2)
+
+    def peer_of(step):
+        return (me_t + step * upper + (nt - step) * (1 - upper)) % nt
+
     def remote(src, dst, send, recv, tm=None, rows=None):
         device = {"tm": me_t if tm is None else tm, "rows": me_r if rows is None else rows}
         return pltpu.make_async_remote_copy(
@@ -263,7 +268,7 @@
         jo, size, run, _ = p.chunks[j]
         out = []
         for step in range(1, nt):
-            peer = (me_t + step) % nt
+            peer = peer_of(step)
             one = w1b.at[me_t, me_r, :, pl.ds(jo, size)]
             two = w2b.at[me_r, pl.ds(pl.multiple_of(jo + run * me_t, run), run), :]
             out.append(remote(one, one, send_sem.at[0, j], ag_sem.at[j, 0], tm=peer))
@@ -385,17 +390,18 @@
     forward_tile(1)
     forward_tiles(2, nb // 4 - 1)
     spread(2)
-    forward_tiles(nb // 4 - 1, nb * 5 // 12)
+    forward_tiles(nb // 4 - 1, nb * 3 // 8)
     gather_one(0)
     spread(3)
     spread(4)
-    forward_tiles(nb * 5 // 12, nb * 7 // 12)
+    forward_tiles(nb * 3 // 8, nb // 2)
     gather_one(1)
-    forward_tiles(nb * 7 // 12, nb * 3 // 4)
+    forward_tiles(nb // 2, nb * 2 // 3)
     gather_two(0)
     arrived(frx.at[pl.ds(HALO + t_len, HALO)], halo_sem.at[1])
-    forward_tiles(nb * 3 // 4, nb)
+    forward_tiles(nb * 2 // 3, nb * 5 // 6)
     gather_two(1)
+    forward_tiles(nb * 5 // 6, nb)
     gather_one(2)
     arrived(frx.at[pl.ds(0, HALO)], halo_sem.at[0])
     forward_tile(0, nb - 1)
@@ -426,7 +432,7 @@
         jo, size, start_row, run = parts_of(j)
         out = []
         for step in range(1, nt):
-            peer = (me_t + step) % nt
+            peer = peer_of(step)
             out.append(remote(r1w1.at[0, peer, :, pl.ds(jo, size)], r3w1.at[me_t, :, pl.ds(jo, size)], send_sem.at[5, j], rs_sem.at[j, 2], tm=peer))
             out.append(remote(r1w2.at[0, pl.ds(pl.multiple_of(jo + run * peer, run), run), :], r3w2.at[me_t, pl.ds(start_row, run), :], send_sem.at[5, j], rs_sem.at[j, 2], tm=peer))
         return out
@@ -557,7 +563,15 @@
             acc2[:, 0:size] = two + jnp.where(i > 0, acc2[:, 0:size], 0.0)
 
     def then(*calls):
-        return [(at, functools.partial(task, j)) for at, task, j in calls]
+        slots = {}
+        for at, task, j in calls:
+            slots.setdefault(at, []).append((task, j))
+
+        def run(tasks):
+            for task, j in tasks:
+                task(j)
+
+        return [(at, functools.partial(run, tasks)) for at, tasks in slots.items()]
 
     main_block(0, then((1, gather_one, 3), (1, spread, 5), (1, spread, 6), (2, gather_two, 2), (2, gather_one, 4)))
     sum_zero(0)
@@ -586,26 +600,25 @@
 
     unit_rows = 2 * TILE
 
-    def backward_dots(u):
+    def backward_dots(u, held):
         size = p.blocks[last][1]
         rows = pl.ds(pl.multiple_of(u * unit_rows, unit_rows), unit_rows)
         w1, w2 = weights_of(last)
-        branch = jnp.dot(nm[rows, 0:size], w2, preferred_element_type=F32)
-        br[rows, :] += branch
-        back = back_dot(gb[rows, 0:size], w1)
-        for s in range(2):
-            for c in range(p.nc):
-                piece = back[TILE * s : TILE * s + TILE, 128 * c : 128 * c + 128]
-                gn[2 * u + s, c, GAP : GAP + TILE, :] += piece
-
-    def backward_tile(b):
+        held[0:unit_rows, :] = jnp.dot(nm[rows, 0:size], w2, preferred_element_type=F32)
+        held[unit_rows : 2 * unit_rows, :] = back_dot(gb[rows, 0:size], w1)
+
+    def backward_tile(b, held, at):
         row = pl.multiple_of(b * TILE, TILE)
         step = 32
         for q in range(TILE // step):
             rows = pl.ds(row + q * step, step)
             place = slice(GAP + q * step, GAP + q * step + step)
-            accs[11] += fold(ct[rows, :].astype(F32) * br[rows, :])
-            grad = jnp.concatenate([gn[b, c, place, :] for c in range(p.nc)], axis=1)
+            share = slice(at + q * step, at + q * step + step)
+            branch = br[rows, :] + held[share, :]
+            br[rows, :] = branch
+            accs[11] += fold(ct[rows, :].astype(F32) * branch)
+            share = slice(unit_rows + at + q * step, unit_rows + at + q * step + step)
+            grad = jnp.concatenate([gn[b, c, place, :] for c in range(p.nc)], axis=1) + held[share, :]
             unit = xhat[rows, :].astype(F32)
             both_of = grad * unit
             accs[8] += fold(both_of)
@@ -634,22 +647,21 @@
             remote(gn.at[0, :, pl.ds(GAP, GAP), :], hnext, send_sem.at[7, 3], halo_sem.at[3], tm=before),
         ]
 
-    backward_dots(0)
+    def backward_unit(u, held):
+        backward_tile(2 * u, held, 0)
+        backward_tile(2 * u + 1, held, TILE)
+
     units = nb // 2
-
-    @pl.loop(0, units - 1)
-    def _(u):
-        for at, task in then(
-            (1, sum_one, 5), (1, sum_one, 6), (2, sum_two, 4), (6, sum_two, 5), (6, sum_three, 3), (8, sum_three, 4), (9, sum_two, 6)
-        ):
-            pl.when(u == at)(task)
-        backward_dots(u + 1)
-        backward_tile(2 * u)
-        backward_tile(2 * u + 1)
-
-    @pl.loop(nb - 2, nb)
-    def _(b):
-        backward_tile(b)
+    backward_dots(0, acc1)
+
+    @pl.loop(0, units // 2)
+    def _(v):
+        for at, task in then((1, sum_one, 5), (1, sum_one, 6), (1, sum_two, 4), (4, sum_two, 5), (4, sum_three, 3), (5, sum_two, 6)):
+            pl.when(v == at)(task)
+        backward_dots(2 * v + 1, acc2)
+        backward_unit(2 * v, acc1)
+        backward_dots(2 * v + 2 - (2 * v + 2) // units, acc1)
+        backward_unit(2 * v + 1, acc2)
 
     start(edge_sends())
 
@@ -676,7 +688,7 @@
     def small_two_sends():
         out = []
         for step in range(1, nt):
-            peer = (me_t + step) % nt
+            peer = peer_of(step)
             out.append(remote(smq.at[nt], smq.at[me_t], send_sem.at[8, 0], sm_sem.at[1], tm=peer))
         return out
 
@@ -736,6 +748,7 @@
 
     cut = [1, 1 + (nb - 2) // 2, 1 + (nb - 2) * 3 // 4, nb - 1]
     last_tiles(cut[0], cut[1])
+    sum_three(4)
     small_two()
     sum_three(5)
     last_tiles(cut[1], cut[2])

time: 80.7 us -> 80.1 us (level)
  no operation moved by 1% of the time
where the time goes in v5:
time: 80.1 us; the launch traced here: 79.9 us
  Pallas kernels  79 us (99%)
  between operations  0.89 us (1%)
    pallas_call x1, Pallas kernels, call(): pl.pallas_call(functools.partial(kernel, plan), out_shape=(v((t, d), BF16...  74.6 us
    pallas_call x1, Pallas kernels, finish(): pl.pallas_call(functools.partial(finish_kernel, plan), out_shape=(whole,...  4.37 us

profile of v5, /device:TPU:0, one launch (start us, length us, event | category | flops | bytes accessed | tf_op | source)
XLA Modules:
  0.0 79.9 jit_solution(10958248784336281437)
XLA Ops:
  0.7 0.0 copy-start
  0.7 0.0 copy-start.3
  0.7 0.0 copy-start.2
  0.7 0.0 copy-start.1
  0.7 74.6 %shard_map.278 = (bf16[3072,512]{1,0:T(8,128)(2,1)S(1)}, bf16[3072,512]{1,0:T(8,128)(2,1)S(1)}, f32[4,16,1536]{2,1,0:T(8,128)S(1)}, f32[4,192,128]{2,1,0:T(8,128...) custom-call(bf16[1,3072,512]{2,1,0:T(8,128)(2,1)} %frames_hbm.1, ...), custom_call_target="tpu_custom_call" | custom-call | tf_op jit(solution)/shard_map/pallas_call | solution.py:926
  75.4 0.0 copy-done
  75.4 0.0 copy-done.3
  75.4 0.0 copy-done.2
  75.4 0.0 copy-done.1
  75.4 4.4 %shard_map.279 = (bf16[1,3072,512]{2,1,0:T(8,128)(2,1)}, bf16[1,3072,512]{2,1,0:T(8,128)(2,1)}, f32[64,1536]{1,0:T(8,128)}, f32[64,1536]{1,0:T(8,128)}, f32[64,1...) custom-call(bf16[3072,512]{1,0:T(8,128)(2,1)S(1)} %get-tuple-element, ...), custom_call_target="tpu_custom_call" | custom-call | tf_op jit(solution)/shard_map/pallas_call | solution.py:858
Async XLA Ops:
  0.7 74.7 %copy-start = (f32[15,512]{1,0:T(8,128)S(1)}, f32[15,512]{1,0:T(8,128)}, u32[]{:S(2)}) copy-start(f32[15,512]{1,0:T(8,128)} %small_master.1) | copy-start | bytes 92164
  0.7 74.7 %copy-start.3 = (f32[15,512]{1,0:T(8,128)S(1)}, f32[15,512]{1,0:T(8,128)}, u32[]{:S(2)}) copy-start(f32[15,512]{1,0:T(8,128)} %small_average.1) | copy-start | bytes 92164
  0.7 74.7 %copy-start.2 = (f32[15,512]{1,0:T(8,128)S(1)}, f32[15,512]{1,0:T(8,128)}, u32[]{:S(2)}) copy-start(f32[15,512]{1,0:T(8,128)} %small_second.1) | copy-start | bytes 92164
  0.7 74.7 %copy-start.1 = (f32[15,512]{1,0:T(8,128)S(1)}, f32[15,512]{1,0:T(8,128)}, u32[]{:S(2)}) copy-start(f32[15,512]{1,0:T(8,128)} %small_first.1) | copy-start | bytes 92164

commit v6 on v5

--- a/solution.py
+++ b/solution.py
@@ -656,13 +656,14 @@
 
     @pl.loop(0, units // 2)
     def _(v):
-        for at, task in then((1, sum_one, 5), (1, sum_one, 6), (1, sum_two, 4), (4, sum_two, 5), (4, sum_three, 3), (5, sum_two, 6)):
+        for at, task in then((1, sum_one, 5), (1, sum_one, 6), (1, sum_two, 4), (4, sum_two, 5), (4, sum_three, 3)):
             pl.when(v == at)(task)
         backward_dots(2 * v + 1, acc2)
         backward_unit(2 * v, acc1)
         backward_dots(2 * v + 2 - (2 * v + 2) // units, acc1)
         backward_unit(2 * v + 1, acc2)
 
+    sum_two(6)
     start(edge_sends())
 
     hidden_tiles = lane_permuted(lambda i: accb[:, 128 * i : 128 * i + 128], p.regrouped, p.ff // 128)

time: 80.1 us -> 80.2 us (level)
  no operation moved by 1% of the time
where the time goes in v6:
time: 80.2 us; the launch traced here: 80 us
  Pallas kernels  79.1 us (99%)
  between operations  0.89 us (1%)
    pallas_call x1, Pallas kernels, call(): pl.pallas_call(functools.partial(kernel, plan), out_shape=(v((t, d), BF16...  74.7 us
    pallas_call x1, Pallas kernels, finish(): pl.pallas_call(functools.partial(finish_kernel, plan), out_shape=(whole,...  4.37 us

profile of v6, /device:TPU:0, one launch (start us, length us, event | category | flops | bytes accessed | tf_op | source)
XLA Modules:
  0.0 80.0 jit_solution(13056667607937289915)
XLA Ops:
  0.7 0.0 copy-start
  0.7 0.0 copy-start.3
  0.7 0.0 copy-start.2
  0.7 0.0 copy-start.1
  0.7 74.7 %shard_map.278 = (bf16[3072,512]{1,0:T(8,128)(2,1)S(1)}, bf16[3072,512]{1,0:T(8,128)(2,1)S(1)}, f32[4,16,1536]{2,1,0:T(8,128)S(1)}, f32[4,192,128]{2,1,0:T(8,128...) custom-call(bf16[1,3072,512]{2,1,0:T(8,128)(2,1)} %frames_hbm.1, ...), custom_call_target="tpu_custom_call" | custom-call | tf_op jit(solution)/shard_map/pallas_call | solution.py:927
  75.4 0.0 copy-done
  75.5 0.0 copy-done.3
  75.5 0.0 copy-done.2
  75.5 0.0 copy-done.1
  75.5 4.4 %shard_map.279 = (bf16[1,3072,512]{2,1,0:T(8,128)(2,1)}, bf16[1,3072,512]{2,1,0:T(8,128)(2,1)}, f32[64,1536]{1,0:T(8,128)}, f32[64,1536]{1,0:T(8,128)}, f32[64,1...) custom-call(bf16[3072,512]{1,0:T(8,128)(2,1)S(1)} %get-tuple-element, ...), custom_call_target="tpu_custom_call" | custom-call | tf_op jit(solution)/shard_map/pallas_call | solution.py:859
Async XLA Ops:
  0.7 74.8 %copy-start = (f32[15,512]{1,0:T(8,128)S(1)}, f32[15,512]{1,0:T(8,128)}, u32[]{:S(2)}) copy-start(f32[15,512]{1,0:T(8,128)} %small_master.1) | copy-start | bytes 92164
  0.7 74.8 %copy-start.3 = (f32[15,512]{1,0:T(8,128)S(1)}, f32[15,512]{1,0:T(8,128)}, u32[]{:S(2)}) copy-start(f32[15,512]{1,0:T(8,128)} %small_average.1) | copy-start | bytes 92164
  0.7 74.8 %copy-start.2 = (f32[15,512]{1,0:T(8,128)S(1)}, f32[15,512]{1,0:T(8,128)}, u32[]{:S(2)}) copy-start(f32[15,512]{1,0:T(8,128)} %small_second.1) | copy-start | bytes 92164
  0.7 74.8 %copy-start.1 = (f32[15,512]{1,0:T(8,128)S(1)}, f32[15,512]{1,0:T(8,128)}, u32[]{:S(2)}) copy-start(f32[15,512]{1,0:T(8,128)} %small_first.1) | copy-start | bytes 92164
